TPU v7x, 256 devices: a whole 4x4x8 slice. The times are simulated.
256 devices in a mesh: grp: 16 (over z, core), mem: 16 (over y, x).
Axes of the slice: x: 4, y: 4, z: 8, core: 2. Of those that a mesh axis runs over, the one named last changes fastest.
Arguments:
- background: bfloat16 [256, 1024, 512], P('mem', 'grp'), may hold values from -6 to 6
- obs_pert: bfloat16 [1024, 2048, 256], P(('grp', 'mem')), may hold values from -24 to 24
- obs_innov: bfloat16 [1024, 2048], P(('grp', 'mem')), may hold values from -6 to 6
- obs_rinv: bfloat16 [1024, 2048], P(('grp', 'mem')), may hold values from 0.25 to 2.5
- obs_pos: bfloat16 [1024, 2048], P(('grp', 'mem')), may hold values from 0 to 1
- obs_count: int32 [1024], P(('grp', 'mem')), may hold values from 1 to 2048, as said below
Outputs:
- analysis: bfloat16 [256, 1024, 512], P('mem', 'grp')
Inputs may be any that keep to these rules, and one draw needn't show every extreme that they name: The observations of patch p sit in its first obs_count[p] slots; the slots after them hold no observation.
All inputs are finite; a program needn't handle non-finite values.
Results may differ from a plain program's by a relative error of at most 0.0058.
Values may be sent and summed in bfloat16 or wider, within the bound.
No kernel may reach another device: no remote copies, remote signals or barrier semaphores. Data moves between devices by JAX's collectives and lax.ppermute only.
A program may use at most 64 MiB of HBM per device.

v0:
```python
import functools
import jax
import jax.numpy as jnp
from jax import lax
from jax.experimental import pallas as pl
from jax.experimental.pallas import tpu as pltpu
from jax.sharding import PartitionSpec as P

NS_STEPS = 8
LOC_SCALE = 0.8
CHUNK = 1024
OFFSETS = (-1, 0, 1)
RING = ("grp", "mem")
VROWS = 8
F32 = jnp.float32
BF16 = jnp.bfloat16


def locality(position, inv_var, offset):
    distance = position - 0.5 - offset
    return inv_var * jnp.exp(-distance * distance / (2.0 * LOC_SCALE * LOC_SCALE))


def chunk_products(place, patch, start, counts, obs, innov, rinv, pos, rows_buf, lhs, acc, accv):
    members = obs.shape[-1]
    depth = rows_buf.shape[1]
    count = counts[patch]
    slot = start + lax.broadcasted_iota(jnp.int32, (1, depth), 1)
    live = slot < count
    lanes = pl.ds(pl.multiple_of(start, depth), depth)
    position = pos[pl.ds(patch, 1), lanes]
    inv_var = jnp.where(live, rinv[pl.ds(patch, 1), lanes], 0.0)
    departure = innov[pl.ds(patch, 1), lanes]
    turned = rows_buf[place].T.astype(F32)
    row = lax.broadcasted_iota(jnp.int32, (4 * VROWS, depth), 0)
    vec_rows = jnp.zeros((4 * VROWS, depth), F32)
    for number, offset in enumerate(OFFSETS):
        weight = locality(position, inv_var, offset)
        lhs[number * members : (number + 1) * members, :] = (turned * weight).astype(BF16)
        moved = weight * departure
        high = moved.astype(BF16).astype(F32)
        vec_rows = jnp.where(row == number * VROWS, high, vec_rows)
        vec_rows = jnp.where(row == number * VROWS + 1, moved - high, vec_rows)
    lhs[3 * members :, :] = vec_rows.astype(BF16)
    product = jnp.dot(lhs[...], rows_buf[place], preferred_element_type=F32)
    first = pl.ds(pl.multiple_of(patch * members, members), 3 * members)
    acc[first, :] += product[: 3 * members]
    first_v = pl.ds(pl.multiple_of(patch * VROWS, VROWS), 3 * VROWS)
    accv[first_v, :] += product[3 * members : 3 * members + 3 * VROWS]


def gram_loop(patches, counts, obs, innov, rinv, pos, rows_buf, sems, lhs, acc, accv):
    depth = rows_buf.shape[1]
    per_patch = obs.shape[1] // depth

    def copy_of(place, patch, start):
        rows = pl.ds(pl.multiple_of(start, depth), depth)
        return pltpu.make_async_copy(obs.at[patch, rows], rows_buf.at[place], sems.at[place])

    first, step = patches[0], patches[1] - patches[0]

    def where_is(place):
        return first + place // per_patch * step, place % per_patch * depth

    for place in range(2 * per_patch):
        patch, start = where_is(place)

        @pl.when(start < counts[patch])
        def _():
            copy_of(place, patch, start).start()

    def body(place, carry):
        patch, start = where_is(place)

        @pl.when(start < counts[patch])
        def _():
            copy_of(place, patch, start).wait()
            chunk_products(
                place, patch, start, counts, obs, innov, rinv, pos, rows_buf, lhs, acc, accv
            )

        return carry

    return lambda: lax.fori_loop(0, 2 * per_patch, body, 0)


def edge_kernel(counts, obs, innov, rinv, pos, send, kept, kept_v, rows_buf, sems, lhs, acc, accv):
    members = obs.shape[-1]
    last = obs.shape[0] - 1
    run = gram_loop((0, last), counts, obs, innov, rinv, pos, rows_buf, sems, lhs, acc, accv)
    acc[...] = jnp.zeros_like(acc)
    accv[...] = jnp.zeros_like(accv)
    run()
    kept[...] = acc[members:-members, :]
    kept_v[...] = accv[VROWS:-VROWS, :]
    row = lax.broadcasted_iota(jnp.int32, (2 * VROWS, members), 0)
    for side, slot in enumerate((0, last + 2)):
        send[side, :members, :] = acc[slot * members : (slot + 1) * members, :].astype(BF16)
        total = (
            accv[slot * VROWS : slot * VROWS + 1, :] + accv[slot * VROWS + 1 : slot * VROWS + 2, :]
        )
        high = total.astype(BF16).astype(F32)
        tail = jnp.where(row == 0, high, jnp.where(row == 1, total - high, 0.0))
        send[side, members:, :] = tail.astype(BF16)


def inner_kernel(
    counts, obs, innov, rinv, pos, kept, kept_v, out, out_v, rows_buf, sems, lhs, acc, accv
):
    members = obs.shape[-1]
    run = gram_loop((1, 2), counts, obs, innov, rinv, pos, rows_buf, sems, lhs, acc, accv)
    acc[members:-members, :] = kept[...]
    accv[VROWS:-VROWS, :] = kept_v[...]
    run()
    out[...] = acc[members:-members, :]
    out_v[...] = accv[VROWS:-VROWS, :]


def gram_call(kernel, name, extra, outs, counts, obs, innov, rinv, pos):
    patches, slots, members = obs.shape
    vmem = pl.BlockSpec(memory_space=pltpu.VMEM)
    pieces = 2 * (slots // CHUNK)
    return pl.pallas_call(
        kernel,
        name=name,
        out_shape=outs,
        in_specs=[
            pl.BlockSpec(memory_space=pltpu.SMEM),
            pl.BlockSpec(memory_space=pl.ANY),
            vmem,
            vmem,
            vmem,
        ]
        + [vmem] * len(extra),
        out_specs=[vmem] * len(outs),
        scratch_shapes=[
            pltpu.VMEM((pieces, CHUNK, members), BF16),
            pltpu.SemaphoreType.DMA((pieces,)),
            pltpu.VMEM((3 * members + 4 * VROWS, CHUNK), BF16),
            pltpu.VMEM(((patches + 2) * members, members), F32),
            pltpu.VMEM(((patches + 2) * VROWS, members), F32),
        ],
        compiler_params=pltpu.CompilerParams(vmem_limit_bytes=32 << 20),
        cost_estimate=pl.CostEstimate(
            flops=6 * 2 * slots * members * members,
            bytes_accessed=2 * slots * members * 2,
            transcendentals=6 * slots,
        ),
    )(counts, obs, innov, rinv, pos, *extra)


def scalar_steps():
    return (2.25, -2.4375, 1.6875, -0.5625, 0.0625)


def root_kernel(gram, gram_v, from_before, from_after, transform, y_dev, z_dev, p_dev, s_dev):
    members = gram.shape[1]
    patches = gram.shape[0] // members
    row = lax.broadcasted_iota(jnp.int32, (members, members), 0)
    col = lax.broadcasted_iota(jnp.int32, (members, members), 1)
    diagonal = row == col

    def times(a, a_s, b, b_s):
        product = jnp.dot(a.astype(BF16), b.astype(BF16), preferred_element_type=F32)
        return product + a_s * b + b_s * a, a_s * b_s

    totals, vecs = [], []
    for t in range(patches):
        here = gram[t * members : (t + 1) * members, :]
        vec = gram_v[t * VROWS : t * VROWS + 1, :] + gram_v[t * VROWS + 1 : t * VROWS + 2, :]
        for side, edge in ((from_before, 0), (from_after, patches - 1)):
            if t == edge:
                here = here + side[:members, :].astype(F32)
                tail = side[members:, :].astype(F32)
                vec = vec + tail[0:1, :] + tail[1:2, :]
        trace = jnp.sum(jnp.where(diagonal, here, 0.0)) + members * (members - 1.0)
        scale = 1.0 / trace
        y_dev[t] = here * scale + jnp.where(diagonal, (members - 1.0) * scale - 1.0 / members, 0.0)
        totals.append(trace)
        vecs.append(vec)
    a0, a1, a2, a3, a4 = scalar_steps()
    y_s, z_s = 1.0 / members, 1.0
    for pair in range(NS_STEPS // 2):
        first, final = pair == 0, pair == NS_STEPS // 2 - 1
        p_s = y_s * z_s
        p2_s = p_s * p_s
        h_s = a2 + a3 * p_s + a4 * p2_s
        q_s = p2_s * h_s + a0 + a1 * p_s
        for t in range(patches):
            p = y_dev[t] if first else times(z_dev[t], z_s, y_dev[t], y_s)[0]
            p_dev[t] = p
        for t in range(patches):
            p = p_dev[t]
            s_dev[t] = times(p, p_s, p, p_s)[0]
        for t in range(patches):
            p, p2 = p_dev[t], s_dev[t]
            s_dev[t] = times(p2, p2_s, a3 * p + a4 * p2, h_s)[0] + a1 * p
        for t in range(patches):
            q = s_dev[t]
            if not final:
                y_dev[t] = times(y_dev[t], y_s, q, q_s)[0]
            z_dev[t] = q if first else times(z_dev[t], z_s, q, q_s)[0]
        y_s, z_s = y_s * q_s, z_s * q_s
    for t in range(patches):
        z = z_dev[t] + jnp.where(diagonal, z_s, 0.0)
        once = jnp.sum(z * vecs[t], axis=1, keepdims=True)
        twice = jnp.sum(z * once, axis=0, keepdims=True)
        scale = lax.rsqrt(jnp.full((1, members), totals[t], F32) / (members - 1.0))
        mean_row = twice / totals[t]
        transform[t] = (z * scale + mean_row).astype(BF16)


def root_call(gram, gram_v, from_before, from_after):
    members = gram.shape[1]
    patches = gram.shape[0] // members
    dev = pltpu.VMEM((patches, members, members), F32)
    return pl.pallas_call(
        root_kernel,
        name="root",
        out_shape=jax.ShapeDtypeStruct((patches, members, members), BF16),
        scratch_shapes=[dev] * 4,
        compiler_params=pltpu.CompilerParams(vmem_limit_bytes=32 << 20),
        cost_estimate=pl.CostEstimate(
            flops=17 * patches * 2 * members**3, bytes_accessed=2 << 20, transcendentals=0
        ),
    )(gram, gram_v, from_before, from_after)


def apply_kernel(transform, state, out):
    shares, patches, local, width = state.shape
    members = shares * local
    for t in range(patches):
        wide = state[:, t].reshape(members, width).astype(F32)
        center = jnp.sum(wide, axis=0, keepdims=True) * (1.0 / members)
        spread = (wide - center).astype(BF16)
        result = jnp.dot(transform[t], spread, preferred_element_type=F32) + center
        out[:, t] = result.astype(BF16).reshape(shares, local, width)


def apply_call(transform, state):
    patches, members, _ = transform.shape
    return pl.pallas_call(
        apply_kernel,
        name="apply",
        out_shape=jax.ShapeDtypeStruct(state.shape, BF16),
        compiler_params=pltpu.CompilerParams(vmem_limit_bytes=32 << 20),
        cost_estimate=pl.CostEstimate(
            flops=2 * members * state.size, bytes_accessed=4 * state.size, transcendentals=0
        ),
    )(transform, state)


def on_device(background, obs_pert, obs_innov, obs_rinv, obs_pos, obs_count):
    patches, slots, members = obs_pert.shape
    local, group_patches, width = background.shape
    shares = members // local
    by_patch = jnp.swapaxes(background, 0, 1)
    state = lax.all_to_all(by_patch, "mem", split_axis=0, concat_axis=0, tiled=True)
    state = state.reshape(shares, patches, local, width)

    innov, rinv, pos = (a.astype(F32) for a in (obs_innov, obs_rinv, obs_pos))
    sums = [
        jax.ShapeDtypeStruct((patches * members, members), F32),
        jax.ShapeDtypeStruct((patches * VROWS, members), F32),
    ]
    edge = [jax.ShapeDtypeStruct((2, members + 2 * VROWS, members), BF16)]
    send, kept, kept_v = gram_call(
        edge_kernel, "edge", (), edge + sums, obs_count, obs_pert, innov, rinv, pos
    )
    size = lax.axis_size(RING)
    up = [(i, (i + 1) % size) for i in range(size)]
    down = [(j, i) for i, j in up]
    from_after = lax.ppermute(send[0], RING, down)
    from_before = lax.ppermute(send[1], RING, up)
    gram, gram_v = gram_call(
        inner_kernel, "inner", (kept, kept_v), sums, obs_count, obs_pert, innov, rinv, pos
    )
    transform = root_call(gram, gram_v, from_before, from_after)
    result = apply_call(transform, state)
    result = result.reshape(group_patches, local, width)
    result = lax.all_to_all(result, "mem", split_axis=0, concat_axis=0, tiled=True)
    return jnp.swapaxes(result, 0, 1)


def solution(mesh):
    return jax.shard_map(
        on_device,
        mesh=mesh,
        in_specs=(
            P("mem", "grp", None),
            P(("grp", "mem"), None, None),
            P(("grp", "mem"), None),
            P(("grp", "mem"), None),
            P(("grp", "mem"), None),
            P(("grp", "mem")),
        ),
        out_specs=P("mem", "grp", None),
        check_vma=False,
    )
```

profile of v0, /device:TPU:96, one launch (start us, length us, event | category | flops | bytes accessed | tf_op | source)
XLA Modules:
  0.0 58.0 jit_solution(10178862084681525010)
XLA Ops:
  0.0 0.0 copy-start.2
  0.0 0.0 copy-start.3
  0.0 0.0 copy-start.4
  0.0 0.0 copy-start.1
  0.0 2.8 %copy.12 = bf16[16,64,512]{2,0,1:T(8,128)(2,1)} copy(bf16[16,64,512]{2,1,0:T(8,128)(2,1)} %param.6) | data formatting | bytes 2097152 | tf_op args[0]
  2.8 7.0 %all-to-all-start = ((bf16[64,16,512]{2,1,0:T(8,128)(2,1)}), bf16[64,16,512]{2,1,0:T(8,128)(2,1)S(1)}, u32[]{:S(2)}, u32[]{:S(2)}) async-start(bf16[64,16,512]{2,1,0:T(8,128)(2,1)} %bitcast.9), calls=%async_computation | async-start | bytes 2097152 | tf_op jit(solution)/shard_map/all_to_all | solution.py:258
  9.9 0.0 copy-done.2
  9.9 0.0 copy-done.3
  9.9 0.0 copy-done.4
  10.0 0.0 copy-done.1
  10.0 0.0 copy-start
  10.0 2.2 %copy-done = bf16[4,2048,256]{2,1,0:T(8,128)(2,1)S(1)} copy-done((bf16[4,2048,256]{2,1,0:T(8,128)(2,1)S(1)}, bf16[4,2048,256]{2,1,0:T(8,128)(2,1)}, u32[]{:S(2)}) %copy-start) | copy-done | bytes 4194328
  12.2 2.9 %edge.1 = (bf16[2,272,256]{2,1,0:T(8,128)(2,1)S(1)}, f32[1024,256]{1,0:T(8,128)S(1)}, f32[32,256]{1,0:T(8,128)S(1)}) custom-call(s32[4]{0:T(128)S(1)} %copy-done.1, bf16[4,2048,256]{2,1,0:T(8,128)(2,1)S(1)} %copy-done, f32[4,2048]{1,0:T(4,128)S(1)} %convert_element_type.9.innov, f32[4,2048]{1,0:T(4,128)S(1)} %convert_element_type.10.rinv, ...), custom_call_target="tpu_custom_call" | custom-call | flops 1610612736 | bytes 2097152 | tf_op jit(solution)/shard_map/edge/pallas_call | solution.py:123
  15.1 2.7 %collective-permute-start = (bf16[272,256]{1,0:T(8,128)(2,1)S(1)}, bf16[272,256]{1,0:T(8,128)(2,1)S(1)}, u32[]{:S(2)}, u32[]{:S(2)}) collective-permute-start(bf16[272,256]{1,0:T(8,128)(2,1)S(1)} %get-tuple-element.16), channel_id=1, source_target_pairs={{0,1},{1,2},{2,3},{3,4},{4,5},{5,6},{6,7},{7,8},{8,9},{9,10},{10,1... | collective-permute-start | bytes 417800 | tf_op jit(solution)/shard_map/ppermute | solution.py:274
  17.8 3.4 %collective-permute-start.1 = (bf16[272,256]{1,0:T(8,128)(2,1)S(1)}, bf16[272,256]{1,0:T(8,128)(2,1)S(1)}, u32[]{:S(2)}, u32[]{:S(2)}) collective-permute-start(bf16[272,256]{1,0:T(8,128)(2,1)S(1)} %get-tuple-element.15), channel_id=1, source_target_pairs={{1,0},{2,1},{3,2},{4,3},{5,4},{6,5},{7,6},{8,7},{9,8},{10,9},{11,1... | collective-permute-start | bytes 417800 | tf_op jit(solution)/shard_map/ppermute | solution.py:273
  21.1 2.2 %inner.1 = (f32[1024,256]{1,0:T(8,128)S(1)}, f32[32,256]{1,0:T(8,128)S(1)}) custom-call(s32[4]{0:T(128)S(1)} %copy-done.1, bf16[4,2048,256]{2,1,0:T(8,128)(2,1)S(1)} %copy-done, f32[4,2048]{1,0:T(4,128)S(1)} %convert_element_type.9.innov, f32[4,2048]{1,0:T(4,128)S(1)} %convert_element_type.10.rinv, f32[4,2048]{1,0:T(4,128)S(1)} %convert_element_type.11.pos, ...), custom_call_target="tpu_custom_call" | custom-call | flops 1610612736 | bytes 2097152 | tf_op jit(solution)/shard_map/inner/pallas_call | solution.py:123
  23.3 1.7 %collective-permute-done.from_before = bf16[272,256]{1,0:T(8,128)(2,1)S(1)} collective-permute-done((bf16[272,256]{1,0:T(8,128)(2,1)S(1)}, bf16[272,256]{1,0:T(8,128)(2,1)S(1)}, u32[]{:S(2)}, u32[]{:S(2)}) %collective-permute-start) | collective-permute-done | bytes 139296 | tf_op jit(solution)/shard_map/ppermute | solution.py:274
  25.0 1.4 %collective-permute-done.1.from_after = bf16[272,256]{1,0:T(8,128)(2,1)S(1)} collective-permute-done((bf16[272,256]{1,0:T(8,128)(2,1)S(1)}, bf16[272,256]{1,0:T(8,128)(2,1)S(1)}, u32[]{:S(2)}, u32[]{:S(2)}) %collective-permute-start.1) | collective-permute-done | bytes 139296 | tf_op jit(solution)/shard_map/ppermute | solution.py:273
  26.4 4.7 %root.1.transform = bf16[4,256,256]{2,1,0:T(8,128)(2,1)S(1)} custom-call(f32[1024,256]{1,0:T(8,128)S(1)} %get-tuple-element.12.gram, f32[32,256]{1,0:T(8,128)S(1)} %get-tuple-element.13.gram_v, bf16[272,256]{1,0:T(8,128)(2,1)S(1)} %collective-permute-done.from_before, bf16[272,256]{1,0:T(8,128)(2,1)S(1)} %collective-permute-done.1.from_after), custom_call_target="tpu_custom_call" | custom-call | flops 2281701376 | bytes 2097152 | tf_op jit(solution)/shard_map/root/pallas_call | solution.py:217
  31.1 0.0 all-to-all-done
  31.2 0.7 %apply.1 = bf16[16,4,16,512]{3,2,1,0:T(8,128)(2,1)S(1)} custom-call(bf16[4,256,256]{2,1,0:T(8,128)(2,1)S(1)} %root.1.transform, bf16[16,4,16,512]{3,2,1,0:T(8,128)(2,1)S(1)} %bitcast.10), custom_call_target="tpu_custom_call" | custom-call | flops 268435456 | bytes 2097152 | tf_op jit(solution)/shard_map/apply/pallas_call | solution.py:242
  31.9 24.6 %all_to_all.10 = bf16[64,16,512]{2,1,0:T(8,128)(2,1)S(1)} all-to-all(bf16[64,16,512]{2,1,0:T(8,128)(2,1)S(1)} %bitcast.11), channel_id=1, replica_groups=mesh['grp'=16,'mem'=16] {'mem'}, dimensions={0} | all-to-all | bytes 2097152 | tf_op jit(solution)/shard_map/all_to_all | solution.py:281
  56.4 1.5 %copy.10 = bf16[16,64,512]{2,1,0:T(8,128)(2,1)} copy(bf16[16,64,512]{2,0,1:T(8,128)(2,1)S(1)} %bitcast.12) | data formatting | bytes 2097152 | tf_op jit(solution)/shard_map/transpose | solution.py:282
  (4 shorter events, 0.0 us)
Async XLA Ops:
  0.0 9.9 %copy-start.2 = (bf16[4,2048]{1,0:T(4,128)(2,1)S(1)}, bf16[4,2048]{1,0:T(4,128)(2,1)}, u32[]{:S(2)}) copy-start(bf16[4,2048]{1,0:T(4,128)(2,1)} %param.9) | copy-start | bytes 49156
  0.0 9.9 %copy-start.3 = (bf16[4,2048]{1,0:T(4,128)(2,1)S(1)}, bf16[4,2048]{1,0:T(4,128)(2,1)}, u32[]{:S(2)}) copy-start(bf16[4,2048]{1,0:T(4,128)(2,1)} %param.10) | copy-start | bytes 49156
  0.0 9.9 %copy-start.4 = (bf16[4,2048]{1,0:T(4,128)(2,1)S(1)}, bf16[4,2048]{1,0:T(4,128)(2,1)}, u32[]{:S(2)}) copy-start(bf16[4,2048]{1,0:T(4,128)(2,1)} %param.8) | copy-start | bytes 49156
  0.0 9.9 %copy-start.1 = (s32[4]{0:T(128)S(1)}, s32[4]{0:T(128)}, u32[]{:S(2)}) copy-start(s32[4]{0:T(128)} %counts.3) | copy-start | bytes 52
  2.8 28.3 %all-to-all-start = ((bf16[64,16,512]{2,1,0:T(8,128)(2,1)}), bf16[64,16,512]{2,1,0:T(8,128)(2,1)S(1)}, u32[]{:S(2)}, u32[]{:S(2)}) async-start(bf16[64,16,512]{2,1,0:T(8,128)(2,1)} %bitcast.9), calls=%async_computation | async-start | bytes 2097152 | tf_op jit(solution)/shard_map/all_to_all | solution.py:258
  10.0 2.2 %copy-start = (bf16[4,2048,256]{2,1,0:T(8,128)(2,1)S(1)}, bf16[4,2048,256]{2,1,0:T(8,128)(2,1)}, u32[]{:S(2)}) copy-start(bf16[4,2048,256]{2,1,0:T(8,128)(2,1)} %obs.3) | copy-start | bytes 12582916
  15.1 9.9 %collective-permute-start = (bf16[272,256]{1,0:T(8,128)(2,1)S(1)}, bf16[272,256]{1,0:T(8,128)(2,1)S(1)}, u32[]{:S(2)}, u32[]{:S(2)}) collective-permute-start(bf16[272,256]{1,0:T(8,128)(2,1)S(1)} %get-tuple-element.16), channel_id=1, source_target_pairs={{0,1},{1,2},{2,3},{3,4},{4,5},{5,6},{6,7},{7,8},{8,9},{9,10},{10,1... | collective-permute-start | bytes 417800 | tf_op jit(solution)/shard_map/ppermute | solution.py:274
  17.8 8.6 %collective-permute-start.1 = (bf16[272,256]{1,0:T(8,128)(2,1)S(1)}, bf16[272,256]{1,0:T(8,128)(2,1)S(1)}, u32[]{:S(2)}, u32[]{:S(2)}) collective-permute-start(bf16[272,256]{1,0:T(8,128)(2,1)S(1)} %get-tuple-element.15), channel_id=1, source_target_pairs={{1,0},{2,1},{3,2},{4,3},{5,4},{6,5},{7,6},{8,7},{9,8},{10,9},{11,1... | collective-permute-start | bytes 417800 | tf_op jit(solution)/shard_map/ppermute | solution.py:273
where the time goes:
time: 58.2 us; the launch traced here: 58 us
  blocking collectives  24.6 us (42%)
  starting transfers between devices  13.1 us (23%)
  Pallas kernels  10.5 us (18%)
  local copies, waits for them, and re-layouts  6.58 us (11%)
  waiting for transfers between devices  3.09 us (5%)
    all_to_all x1, blocking collectives, on_device(): lax.all_to_all(result, 'mem', split_axis=0, concat_axis=0, tiled=True)  24.6 us
    all_to_all x1, starting transfers between devices, on_device(): lax.all_to_all(by_patch, 'mem', split_axis=0, concat_axis=0, tiled=True)  7.03 us
    pallas_call x2, Pallas kernels, gram_call(): pl.pallas_call(kernel, name=name, out_shape=outs, in_specs=[pl.BlockSpec(...  5.07 us
    unnamed x11, local copies, waits for them, and re-layouts  5.01 us
    pallas_call x1, Pallas kernels, root_call(): pl.pallas_call(root_kernel, name='root', out_shape=jax.ShapeDtypeStruct((...  4.74 us
    ppermute x1, starting transfers between devices, on_device(): from_after = lax.ppermute(send[0], RING, down)  3.37 us
    ppermute x1, starting transfers between devices, on_device(): from_before = lax.ppermute(send[1], RING, up)  2.67 us
    ppermute x1, waiting for transfers between devices, on_device(): from_before = lax.ppermute(send[1], RING, up)  1.66 us
  transfers between devices with their start and end apart: 3, of which 2 were waited for; matrix products, arithmetic and copies ran while one was open for 0% of the time, Pallas kernels for 17%

commit v1 on v0

v1 whole, which is shorter than its diff:
```python
import jax
import jax.numpy as jnp
from jax import lax
from jax.experimental import pallas as pl
from jax.experimental.pallas import tpu as pltpu
from jax.sharding import PartitionSpec as P

NS_STEPS = 8
LOC_SCALE = 0.8
CHUNK = 1024
OFFSETS = (-1, 0, 1)
RING = ("grp", "mem")
VROWS = 8
LANES = 128
MOST_VMEM = 40 << 20
F32 = jnp.float32
BF16 = jnp.bfloat16


def in_hbm(array):
    return pltpu.with_memory_space_constraint(array, pltpu.HBM)


def locality(position, inv_var, offset):
    distance = position - 0.5 - offset
    return inv_var * jnp.exp(-distance * distance / (2.0 * LOC_SCALE * LOC_SCALE))


def chunk_products(place, patch, start, offsets, slot, counts, fields, rows_buf, lhs, acc, accv):
    depth, members = rows_buf.shape[1:]
    span = len(offsets)
    live = start + lax.broadcasted_iota(jnp.int32, (1, depth), 1) < counts[patch]
    lanes = pl.ds(pl.multiple_of(start, depth), depth)
    position = fields[2, pl.ds(patch, 1), lanes]
    inv_var = jnp.where(live, fields[1, pl.ds(patch, 1), lanes], 0.0)
    departure = fields[0, pl.ds(patch, 1), lanes]
    turned = rows_buf[place].T.astype(F32)
    row = lax.broadcasted_iota(jnp.int32, (4 * VROWS, depth), 0)
    vec_rows = jnp.zeros((4 * VROWS, depth), F32)
    for number, offset in enumerate(offsets):
        weight = locality(position, inv_var, offset)
        lhs[number * members : (number + 1) * members, :] = (turned * weight).astype(BF16)
        moved = weight * departure
        high = moved.astype(BF16).astype(F32)
        vec_rows = jnp.where(row == number * VROWS, high, vec_rows)
        vec_rows = jnp.where(row == number * VROWS + 1, moved - high, vec_rows)
    lhs[span * members : span * members + 4 * VROWS, :] = vec_rows.astype(BF16)
    product = jnp.dot(
        lhs[: span * members + 4 * VROWS, :], rows_buf[place], preferred_element_type=F32
    )
    first = pl.ds(pl.multiple_of(slot * members, members), span * members)
    acc[first, :] += product[: span * members]
    first_v = pl.ds(pl.multiple_of(slot * VROWS, VROWS), span * VROWS)
    accv[first_v, :] += product[span * members : span * members + span * VROWS]


def start_rows(pairs, given_counts, counts, count_sem, obs, rows_buf, sems):
    depth = rows_buf.shape[1]
    per_patch = obs.shape[1] // depth
    order = []
    for first, step, base in pairs:
        for place in range(2 * per_patch):
            patch, start = first + place // per_patch * step, place % per_patch * depth
            order.append((patch, start, base + place))

    def begin(patch, start, place):
        pltpu.make_async_copy(
            obs.at[patch, pl.ds(start, depth)], rows_buf.at[place], sems.at[place]
        ).start()

    fetch = pltpu.make_async_copy(given_counts, counts, count_sem)
    fetch.start()
    for patch, start, place in order:
        if start == 0:
            begin(patch, start, place)
    fetch.wait()
    for patch, start, place in order:
        if start > 0:
            pl.when(start < counts[patch])(lambda a=(patch, start, place): begin(*a))


def add_rows(first, step, base, offsets_of, slot_of, counts, obs, fields, bufs):
    rows_buf, sems, lhs, acc, accv = bufs
    depth = rows_buf.shape[1]
    per_patch = obs.shape[1] // depth

    def body(place, carry):
        which = place // per_patch
        patch, start = first + which * step, place % per_patch * depth

        @pl.when(start < counts[patch])
        def _():
            rows = pl.ds(pl.multiple_of(start, depth), depth)
            pltpu.make_async_copy(
                obs.at[patch, rows], rows_buf.at[base + place], sems.at[base + place]
            ).wait()
            chunk_products(
                base + place,
                patch,
                start,
                offsets_of(which),
                slot_of(which),
                counts,
                fields,
                rows_buf,
                lhs,
                acc,
                accv,
            )

        return carry

    lax.fori_loop(0, 2 * per_patch, body, 0)


def by_patch_kernel(
    back, innov, rinv, pos, turned, fields, rows_in, rows_out, narrow, in_sems, out_sems, sems
):
    step = rows_in.shape[2]
    pieces = rows_in.shape[0]

    def fetch(piece):
        return pltpu.make_async_copy(
            back.at[:, pl.ds(piece * step, step)], rows_in.at[piece], in_sems.at[piece]
        )

    def put(piece):
        return pltpu.make_async_copy(
            rows_out.at[piece], turned.at[pl.ds(piece * step, step)], out_sems.at[piece]
        )

    for piece in range(pieces):
        fetch(piece).start()
    loads = [
        pltpu.make_async_copy(field, narrow.at[number], sems.at[number])
        for number, field in enumerate((innov, rinv, pos))
    ]
    for load in loads:
        load.start()
    for piece in range(pieces):
        fetch(piece).wait()
        for first in range(0, rows_in.shape[3], LANES):
            lanes = slice(first, first + LANES)
            for row in range(0, step, 8):
                block = rows_in[piece, :, row : row + 8, lanes]
                rows_out[piece, row : row + 8, :, lanes] = jnp.swapaxes(block, 0, 1)
        put(piece).start()
    for number, load in enumerate(loads):
        load.wait()
        fields[number] = narrow[number].astype(F32)
    for piece in range(pieces):
        put(piece).wait()


def by_patch_call(background, innov, rinv, pos):
    local, group_patches, width = background.shape
    pieces, step = 4, group_patches // 4
    hbm = pl.BlockSpec(memory_space=pltpu.HBM)
    return pl.pallas_call(
        by_patch_kernel,
        name="by_patch",
        out_shape=[
            jax.ShapeDtypeStruct((group_patches, local, width), BF16),
            pltpu.VMEM((3,) + innov.shape, F32),
        ],
        in_specs=[hbm] * 4,
        out_specs=[hbm, pl.BlockSpec(memory_space=pltpu.VMEM)],
        scratch_shapes=[
            pltpu.VMEM((pieces, local, step, width), BF16),
            pltpu.VMEM((pieces, step, local, width), BF16),
            pltpu.VMEM((3,) + innov.shape, BF16),
            pltpu.SemaphoreType.DMA((pieces,)),
            pltpu.SemaphoreType.DMA((pieces,)),
            pltpu.SemaphoreType.DMA((3,)),
        ],
        compiler_params=pltpu.CompilerParams(vmem_limit_bytes=MOST_VMEM),
        cost_estimate=pl.CostEstimate(
            flops=0, bytes_accessed=4 * background.size, transcendentals=0
        ),
    )(in_hbm(background), in_hbm(innov), in_hbm(rinv), in_hbm(pos))


def edge_kernel(
    given_counts, obs, fields, down, up, counts, count_sem, rows_buf, sems, lhs, acc, accv
):
    patches, _, members = obs.shape
    start_rows([(0, patches - 1, 0)], given_counts, counts, count_sem, obs, rows_buf, sems)
    acc[...] = jnp.zeros_like(acc)
    accv[...] = jnp.zeros_like(accv)
    add_rows(
        0,
        patches - 1,
        0,
        lambda which: (2.0 * which.astype(F32) - 1.0,),
        lambda which: which,
        counts,
        obs,
        fields,
        (rows_buf, sems, lhs, acc, accv),
    )
    row = lax.broadcasted_iota(jnp.int32, (2 * VROWS, members), 0)
    for side, send in enumerate((down, up)):
        send[:members, :] = acc[side * members : (side + 1) * members, :].astype(BF16)
        total = accv[side * VROWS : side * VROWS + 1] + accv[side * VROWS + 1 : side * VROWS + 2]
        high = total.astype(BF16).astype(F32)
        tail = jnp.where(row == 0, high, jnp.where(row == 1, total - high, 0.0))
        send[members:, :] = tail.astype(BF16)


def inner_kernel(
    given_counts, obs, fields, transform, gram, gram_v, counts, count_sem, rows_buf, sems, lhs, acc,
    accv, y_dev, z_dev, p_dev, s_dev
):
    patches, slots, members = obs.shape
    base = 2 * (slots // rows_buf.shape[1])
    pairs = [(1, 1, 0), (0, patches - 1, base)]
    start_rows(pairs, given_counts, counts, count_sem, obs, rows_buf, sems)
    acc[...] = jnp.zeros_like(acc)
    accv[...] = jnp.zeros_like(accv)
    bufs = (rows_buf, sems, lhs, acc, accv)
    add_rows(1, 1, 0, lambda which: OFFSETS, lambda which: which, counts, obs, fields, bufs)
    add_rows(
        0,
        patches - 1,
        base,
        lambda which: (0.0 - which.astype(F32), 1.0 - which.astype(F32)),
        lambda which: which * (patches - 2),
        counts,
        obs,
        fields,
        bufs,
    )
    grams, vecs = [], []
    for t in range(1, patches - 1):
        grams.append(acc[t * members : (t + 1) * members, :])
        vecs.append(accv[t * VROWS : t * VROWS + 1, :] + accv[t * VROWS + 1 : t * VROWS + 2, :])
    for side, t in enumerate((0, patches - 1)):
        gram[side] = acc[t * members : (t + 1) * members, :]
        gram_v[side] = accv[t * VROWS : (t + 1) * VROWS, :]
    root_into(transform, grams, vecs, y_dev, z_dev, p_dev, s_dev)


def gram_call(kernel, name, outs, span, targets, chunks, scratch, flops, counts, obs, fields):
    patches, slots, members = obs.shape
    hbm, vmem = (pl.BlockSpec(memory_space=space) for space in (pltpu.HBM, pltpu.VMEM))
    return pl.pallas_call(
        kernel,
        name=name,
        out_shape=outs,
        in_specs=[hbm, hbm, vmem],
        out_specs=[vmem] * len(outs),
        scratch_shapes=[
            pltpu.SMEM((patches,), jnp.int32),
            pltpu.SemaphoreType.DMA,
            pltpu.VMEM((chunks, CHUNK, members), BF16),
            pltpu.SemaphoreType.DMA((chunks,)),
            pltpu.VMEM((span * members + 4 * VROWS, CHUNK), BF16),
            pltpu.VMEM((targets * members, members), F32),
            pltpu.VMEM((targets * VROWS, members), F32),
        ]
        + scratch,
        compiler_params=pltpu.CompilerParams(vmem_limit_bytes=MOST_VMEM),
        cost_estimate=pl.CostEstimate(
            flops=flops, bytes_accessed=2 * slots * members * 2, transcendentals=6 * slots
        ),
    )(in_hbm(counts), in_hbm(obs), fields)


def scalar_steps():
    return (2.25, -2.4375, 1.6875, -0.5625, 0.0625)


def root_into(transform, grams, vecs, y_dev, z_dev, p_dev, s_dev, between=lambda: None):
    patches = len(grams)
    members = grams[0].shape[1]
    row = lax.broadcasted_iota(jnp.int32, (members, members), 0)
    col = lax.broadcasted_iota(jnp.int32, (members, members), 1)
    diagonal = row == col

    def times(a, a_s, b, b_s):
        product = jnp.dot(a.astype(BF16), b.astype(BF16), preferred_element_type=F32)
        return product + a_s * b + b_s * a

    totals = []
    for t, here in enumerate(grams):
        trace = jnp.sum(jnp.where(diagonal, here, 0.0)) + members * (members - 1.0)
        scale = 1.0 / trace
        y_dev[t] = here * scale + jnp.where(diagonal, (members - 1.0) * scale - 1.0 / members, 0.0)
        totals.append(trace)
    a0, a1, a2, a3, a4 = scalar_steps()
    y_s, z_s = 1.0 / members, 1.0
    for pair in range(NS_STEPS // 2):
        first, final = pair == 0, pair == NS_STEPS // 2 - 1
        p_s = y_s * z_s
        p2_s = p_s * p_s
        h_s = a2 + a3 * p_s + a4 * p2_s
        q_s = p2_s * h_s + a0 + a1 * p_s
        for t in range(patches):
            p_dev[t] = y_dev[t] if first else times(z_dev[t], z_s, y_dev[t], y_s)
        between()
        for t in range(patches):
            s_dev[t] = times(p_dev[t], p_s, p_dev[t], p_s)
        between()
        for t in range(patches):
            p, p2 = p_dev[t], s_dev[t]
            s_dev[t] = times(p2, p2_s, a3 * p + a4 * p2, h_s) + a1 * p
        for t in range(patches):
            q = s_dev[t]
            if not final:
                y_dev[t] = times(y_dev[t], y_s, q, q_s)
            z_dev[t] = q if first else times(z_dev[t], z_s, q, q_s)
        y_s, z_s = y_s * q_s, z_s * q_s
    for t in range(patches):
        z = z_dev[t] + jnp.where(diagonal, z_s, 0.0)
        once = jnp.sum(z * vecs[t], axis=1, keepdims=True)
        twice = jnp.sum(z * once, axis=0, keepdims=True)
        scale = lax.rsqrt(jnp.full((1, members), totals[t], F32) / (members - 1.0))
        transform[t] = (z * scale + twice / totals[t]).astype(BF16)


def apply_to(transform, t, state, out, lanes):
    shares, _, local, _ = state.shape
    wide = state[:, t, :, lanes].astype(F32).reshape(shares * local, LANES)
    center = jnp.sum(wide, axis=0, keepdims=True) * (1.0 / (shares * local))
    spread = (wide - center).astype(BF16)
    result = jnp.dot(transform, spread, preferred_element_type=F32) + center
    out[:, t, :, lanes] = result.astype(BF16).reshape(shares, local, LANES)


def outer_kernel(
    inner, gram, gram_v, from_before, from_after, state, out, transform, y_dev, z_dev, p_dev, s_dev
):
    members = gram.shape[1]
    patches, width = state.shape[1], state.shape[3]
    grams, vecs = [], []
    for t, side in enumerate((from_before, from_after)):
        tail = side[members:, :].astype(F32)
        grams.append(gram[t] + side[:members, :].astype(F32))
        vecs.append(gram_v[t, 0:1, :] + gram_v[t, 1:2, :] + tail[0:1, :] + tail[1:2, :])
    columns = [slice(first, first + LANES) for first in range(0, width, LANES)]
    fill = [(t, lanes) for t in range(1, patches - 1) for lanes in columns]

    def between():
        if fill:
            t, lanes = fill.pop(0)
            apply_to(inner[t - 1], t, state, out, lanes)

    root_into(transform, grams, vecs, y_dev, z_dev, p_dev, s_dev, between)
    while fill:
        between()
    for lanes in columns:
        for side, t in enumerate((0, patches - 1)):
            apply_to(transform[side], t, state, out, lanes)


def outer_call(inner, gram, gram_v, from_before, from_after, state):
    patches, members, _ = gram.shape
    dev = pltpu.VMEM((patches, members, members), F32)
    return pl.pallas_call(
        outer_kernel,
        name="outer",
        out_shape=jax.ShapeDtypeStruct(state.shape, BF16),
        scratch_shapes=[pltpu.VMEM((patches, members, members), BF16)] + [dev] * 4,
        compiler_params=pltpu.CompilerParams(vmem_limit_bytes=40 << 20),
        cost_estimate=pl.CostEstimate(
            flops=17 * patches * 2 * members**3 + 2 * members * state.size,
            bytes_accessed=4 * state.size,
            transcendentals=0,
        ),
    )(inner, gram, gram_v, from_before, from_after, state)


def on_device(background, obs_pert, obs_innov, obs_rinv, obs_pos, obs_count):
    patches, slots, members = obs_pert.shape
    local, group_patches, width = background.shape
    shares = members // local
    pieces = slots // CHUNK
    matmul = 2 * slots * members * members
    by_patch, fields = by_patch_call(background, obs_innov, obs_rinv, obs_pos)
    given = (obs_count, obs_pert, fields)
    state = lax.all_to_all(by_patch, "mem", split_axis=0, concat_axis=0, tiled=True)
    state = state.reshape(shares, patches, local, width)
    to_before, to_after = gram_call(
        edge_kernel,
        "edge",
        [pltpu.VMEM((members + 2 * VROWS, members), BF16)] * 2,
        1,
        2,
        2 * pieces,
        [],
        2 * matmul,
        *given,
    )
    size = lax.axis_size(RING)
    up = [(i, (i + 1) % size) for i in range(size)]
    down = [(j, i) for i, j in up]
    from_after = lax.ppermute(to_before, RING, down)
    from_before = lax.ppermute(to_after, RING, up)
    inner, gram, gram_v = gram_call(
        inner_kernel,
        "inner",
        [
            pltpu.VMEM((patches - 2, members, members), BF16),
            pltpu.VMEM((2, members, members), F32),
            pltpu.VMEM((2, VROWS, members), F32),
        ],
        3,
        patches,
        4 * pieces,
        [pltpu.VMEM((patches - 2, members, members), F32)] * 4,
        10 * matmul,
        *given,
    )
    result = outer_call(inner, gram, gram_v, from_before, from_after, state)
    result = result.reshape(group_patches, local, width)
    result = lax.all_to_all(result, "mem", split_axis=0, concat_axis=0, tiled=True)
    return jnp.swapaxes(result, 0, 1)


def solution(mesh):
    return jax.shard_map(
        on_device,
        mesh=mesh,
        in_specs=(
            P("mem", "grp", None),
            P(("grp", "mem"), None, None),
            P(("grp", "mem"), None),
            P(("grp", "mem"), None),
            P(("grp", "mem"), None),
            P(("grp", "mem")),
        ),
        out_specs=P("mem", "grp", None),
        check_vma=False,
    )
```

time: 58.2 us -> 55.6 us (0.955)
  local copies, waits for them, and re-layouts: 6.58 us -> 1.55 us
  Pallas kernels: 10.5 us -> 15 us
  blocking collectives: 24.6 us -> 22.1 us
    unnamed x11 -> x0, local copies, waits for them, and re-layouts: 5.01 us -> none
    pallas_call x4, Pallas kernels: 10.5 us -> 15 us  [the longest x2 8.96 us: gram_call(): pl.pallas_call(kernel, name=name, out_shape=outs, in_specs=[hbm, hbm, vme...]
    all_to_all x1, blocking collectives: 24.6 us -> 22.1 us  [on_device(): lax.all_to_all(result, 'mem', split_axis=0, concat_axis=0, tiled=True)]
    all_to_all x1, waiting for transfers between devices: 0.01 us -> 2 us  [on_device(): lax.all_to_all(by_patch, 'mem', split_axis=0, concat_axis=0, tiled=True)]
    ppermute x2, waiting for transfers between devices: 3.08 us -> 1.49 us  [the longest x1 1.49 us: on_device(): from_after = lax.ppermute(to_before, RING, down)]
  transfers between devices with their start and end apart: 3 -> 3, of which waited for: 2 -> 2; matrix products, arithmetic and copies ran while one was open for 0% -> 0% of each run, Pallas kernels for 17% -> 16%
where the time goes in v1:
time: 55.6 us; the launch traced here: 55.3 us
  blocking collectives  22.1 us (40%)
  Pallas kernels  15 us (27%)
  starting transfers between devices  13.1 us (24%)
  waiting for transfers between devices  3.5 us (6%)
  local copies, waits for them, and re-layouts  1.55 us (3%)
    all_to_all x1, blocking collectives, on_device(): lax.all_to_all(result, 'mem', split_axis=0, concat_axis=0, tiled=True)  22.1 us
    pallas_call x2, Pallas kernels, gram_call(): pl.pallas_call(kernel, name=name, out_shape=outs, in_specs=[hbm, hbm, vme...  8.96 us
    all_to_all x1, starting transfers between devices, on_device(): lax.all_to_all(by_patch, 'mem', split_axis=0, concat_axis=0, tiled=True)  7.05 us
    ppermute x1, starting transfers between devices, on_device(): from_after = lax.ppermute(to_before, RING, down)  4.04 us
    pallas_call x1, Pallas kernels, outer_call(): pl.pallas_call(outer_kernel, name='outer', out_shape=jax.ShapeDtypeStruct...  3.96 us
    pallas_call x1, Pallas kernels, by_patch_call(): pl.pallas_call(by_patch_kernel, name='by_patch', out_shape=[jax.ShapeDtyp...  2.1 us
    all_to_all x1, waiting for transfers between devices, on_device(): lax.all_to_all(by_patch, 'mem', split_axis=0, concat_axis=0, tiled=True)  2 us
    ppermute x1, starting transfers between devices, on_device(): from_before = lax.ppermute(to_after, RING, up)  2 us
  transfers between devices with their start and end apart: 3, of which 2 were waited for; matrix products, arithmetic and copies ran while one was open for 0% of the time, Pallas kernels for 16%

profile of v1, /device:TPU:96, one launch (start us, length us, event | category | flops | bytes accessed | tf_op | source)
XLA Modules:
  0.0 55.3 jit_solution(4970072578180361308)
XLA Ops:
  0.0 2.1 %by_patch.1 = (bf16[64,16,512]{2,1,0:T(8,128)(2,1)}, f32[3,4,2048]{2,1,0:T(4,128)S(1)}) custom-call(bf16[16,64,512]{2,1,0:T(8,128)(2,1)} %back.1, bf16[4,2048]{1,0:T(4,128)(2,1)} %innov.1, bf16[4,2048]{1,0:T(4,128)(2,1)} %rinv.1, bf16[4,2048]{1,0:T(4,128)(2,1)} %pos.1), custom_call_target="tpu_custom_call" | custom-call | bytes 2097152 | tf_op jit(solution)/shard_map/by_patch/pallas_call | solution.py:159
  2.1 7.0 %all-to-all-start = ((bf16[64,16,512]{2,1,0:T(8,128)(2,1)}), bf16[64,16,512]{2,1,0:T(8,128)(2,1)S(1)}, u32[]{:S(2)}, u32[]{:S(2)}) async-start(bf16[64,16,512]{2,1,0:T(8,128)(2,1)} %get-tuple-element.18), calls=%async_computation | async-start | bytes 2097152 | tf_op jit(solution)/shard_map/all_to_all | solution.py:381
  9.2 1.9 %edge.1 = (bf16[272,256]{1,0:T(8,128)(2,1)S(1)}, bf16[272,256]{1,0:T(8,128)(2,1)S(1)}) custom-call(s32[4]{0:T(128)} %given_counts.3, bf16[4,2048,256]{2,1,0:T(8,128)(2,1)} %obs.3, f32[3,4,2048]{2,1,0:T(4,128)S(1)} %get-tuple-element.12.fields), custom_call_target="tpu_custom_call" | custom-call | flops 536870912 | bytes 2097152 | tf_op jit(solution)/shard_map/edge/pallas_call | solution.py:246
  11.1 2.0 %collective-permute-start = (bf16[272,256]{1,0:T(8,128)(2,1)S(1)}, bf16[272,256]{1,0:T(8,128)(2,1)S(1)}, u32[]{:S(2)}, u32[]{:S(2)}) collective-permute-start(bf16[272,256]{1,0:T(8,128)(2,1)S(1)} %get-tuple-element.16), channel_id=1, source_target_pairs={{0,1},{1,2},{2,3},{3,4},{4,5},{5,6},{6,7},{7,8},{8,9},{9,10},{10,1... | collective-permute-start | bytes 417800 | tf_op jit(solution)/shard_map/ppermute | solution.py:398
  13.1 4.0 %collective-permute-start.1 = (bf16[272,256]{1,0:T(8,128)(2,1)S(1)}, bf16[272,256]{1,0:T(8,128)(2,1)S(1)}, u32[]{:S(2)}, u32[]{:S(2)}) collective-permute-start(bf16[272,256]{1,0:T(8,128)(2,1)S(1)} %get-tuple-element.17), channel_id=1, source_target_pairs={{1,0},{2,1},{3,2},{4,3},{5,4},{6,5},{7,6},{8,7},{9,8},{10,9},{11,1... | collective-permute-start | bytes 417800 | tf_op jit(solution)/shard_map/ppermute | solution.py:397
  17.1 7.0 %inner.1 = (bf16[2,256,256]{2,1,0:T(8,128)(2,1)S(1)}, f32[2,256,256]{2,1,0:T(8,128)S(1)}, f32[2,8,256]{2,1,0:T(8,128)S(1)}) custom-call(s32[4]{0:T(128)} %given_counts.3, bf16[4,2048,256]{2,1,0:T(8,128)(2,1)} %obs.3, f32[3,4,2048]{2,1,0:T(4,128)S(1)} %get-tuple-element.12.fields), custom_call_target="tpu_custom_call" | custom-call | flops 2684354560 | bytes 2097152 | tf_op jit(solution)/shard_map/inner/pallas_call | solution.py:246
  24.2 0.0 collective-permute-done.from_before
  24.2 1.5 %collective-permute-done.1.from_after = bf16[272,256]{1,0:T(8,128)(2,1)S(1)} collective-permute-done((bf16[272,256]{1,0:T(8,128)(2,1)S(1)}, bf16[272,256]{1,0:T(8,128)(2,1)S(1)}, u32[]{:S(2)}, u32[]{:S(2)}) %collective-permute-start.1) | collective-permute-done | bytes 139296 | tf_op jit(solution)/shard_map/ppermute | solution.py:397
  25.7 2.0 %all-to-all-done = bf16[64,16,512]{2,1,0:T(8,128)(2,1)S(1)} async-done(((bf16[64,16,512]{2,1,0:T(8,128)(2,1)}), bf16[64,16,512]{2,1,0:T(8,128)(2,1)S(1)}, u32[]{:S(2)}, u32[]{:S(2)}) %all-to-all-start) | async-done | bytes 1048608 | tf_op jit(solution)/shard_map/all_to_all | solution.py:381
  27.7 4.0 %outer.1 = bf16[16,4,16,512]{3,2,1,0:T(8,128)(2,1)S(1)} custom-call(bf16[2,256,256]{2,1,0:T(8,128)(2,1)S(1)} %get-tuple-element.13.inner, f32[2,256,256]{2,1,0:T(8,128)S(1)} %get-tuple-element.14.gram, f32[2,8,256]{2,1,0:T(8,128)S(1)} %get-tuple-element.15.gram_v, bf16[272,256]{1,0:T(8,128)(2,1)S(1)} %collective-permute-done.from_before, ...), custom_call_target="tpu_custom_call" | custom-call | flops 1409286144 | bytes 2097152 | tf_op jit(solution)/shard_map/outer/pallas_call | solution.py:359
  31.7 22.1 %all_to_all.10 = bf16[64,16,512]{2,1,0:T(8,128)(2,1)S(1)} all-to-all(bf16[64,16,512]{2,1,0:T(8,128)(2,1)S(1)} %bitcast.4), channel_id=1, replica_groups=mesh['grp'=16,'mem'=16] {'mem'}, dimensions={0} | all-to-all | bytes 2097152 | tf_op jit(solution)/shard_map/all_to_all | solution.py:416
  53.8 1.5 %copy.8 = bf16[16,64,512]{2,1,0:T(8,128)(2,1)} copy(bf16[16,64,512]{2,0,1:T(8,128)(2,1)S(1)} %bitcast.5) | data formatting | bytes 2097152 | tf_op jit(solution)/shard_map/transpose | solution.py:417
Async XLA Ops:
  2.1 25.6 %all-to-all-start = ((bf16[64,16,512]{2,1,0:T(8,128)(2,1)}), bf16[64,16,512]{2,1,0:T(8,128)(2,1)S(1)}, u32[]{:S(2)}, u32[]{:S(2)}) async-start(bf16[64,16,512]{2,1,0:T(8,128)(2,1)} %get-tuple-element.18), calls=%async_computation | async-start | bytes 2097152 | tf_op jit(solution)/shard_map/all_to_all | solution.py:381
  11.1 13.1 %collective-permute-start = (bf16[272,256]{1,0:T(8,128)(2,1)S(1)}, bf16[272,256]{1,0:T(8,128)(2,1)S(1)}, u32[]{:S(2)}, u32[]{:S(2)}) collective-permute-start(bf16[272,256]{1,0:T(8,128)(2,1)S(1)} %get-tuple-element.16), channel_id=1, source_target_pairs={{0,1},{1,2},{2,3},{3,4},{4,5},{5,6},{6,7},{7,8},{8,9},{9,10},{10,1... | collective-permute-start | bytes 417800 | tf_op jit(solution)/shard_map/ppermute | solution.py:398
  13.1 12.6 %collective-permute-start.1 = (bf16[272,256]{1,0:T(8,128)(2,1)S(1)}, bf16[272,256]{1,0:T(8,128)(2,1)S(1)}, u32[]{:S(2)}, u32[]{:S(2)}) collective-permute-start(bf16[272,256]{1,0:T(8,128)(2,1)S(1)} %get-tuple-element.17), channel_id=1, source_target_pairs={{1,0},{2,1},{3,2},{4,3},{5,4},{6,5},{7,6},{8,7},{9,8},{10,9},{11,1... | collective-permute-start | bytes 417800 | tf_op jit(solution)/shard_map/ppermute | solution.py:397

commit v2 on v1

--- a/solution.py
+++ b/solution.py
@@ -154,7 +154,7 @@
 
 def by_patch_call(background, innov, rinv, pos):
     local, group_patches, width = background.shape
-    pieces, step = 4, group_patches // 4
+    pieces, step = 8, group_patches // 8
     hbm = pl.BlockSpec(memory_space=pltpu.HBM)
     return pl.pallas_call(
         by_patch_kernel,
@@ -181,7 +181,7 @@
 
 
 def edge_kernel(
-    given_counts, obs, fields, down, up, counts, count_sem, rows_buf, sems, lhs, acc, accv
+    given_counts, obs, fields, near, far, counts, count_sem, rows_buf, sems, lhs, acc, accv
 ):
     patches, _, members = obs.shape
     start_rows([(0, patches - 1, 0)], given_counts, counts, count_sem, obs, rows_buf, sems)
@@ -198,13 +198,48 @@
         fields,
         (rows_buf, sems, lhs, acc, accv),
     )
-    row = lax.broadcasted_iota(jnp.int32, (2 * VROWS, members), 0)
-    for side, send in enumerate((down, up)):
-        send[:members, :] = acc[side * members : (side + 1) * members, :].astype(BF16)
-        total = accv[side * VROWS : side * VROWS + 1] + accv[side * VROWS + 1 : side * VROWS + 2]
-        high = total.astype(BF16).astype(F32)
-        tail = jnp.where(row == 0, high, jnp.where(row == 1, total - high, 0.0))
-        send[members:, :] = tail.astype(BF16)
+    odd = lax.rem(lax.axis_index(RING[1]), 2)
+    for side, send in ((1 - odd, near), (odd, far)):
+        sums = accv[pl.ds(pl.multiple_of(side * VROWS, VROWS), VROWS), :]
+        pack(acc.at[pl.ds(pl.multiple_of(side * members, members), members)], sums, send)
+
+
+def half_masks(half):
+    row = lax.broadcasted_iota(jnp.int32, (half, half), 0)
+    col = lax.broadcasted_iota(jnp.int32, (half, half), 1)
+    return row, col
+
+
+def pack(gram, sums, send):
+    members = gram.shape[1]
+    half = members // 2
+    row, col = half_masks(half)
+    low = gram[half:, half:]
+    send[:half, :half] = jnp.where(col >= row, gram[:half, :half], low).astype(BF16)
+    send[:half, half:] = gram[:half, half:].astype(BF16)
+    diagonal = jnp.sum(jnp.where(row == col, low, 0.0), axis=0, keepdims=True)
+    total = sums[0:1] + sums[1:2]
+    high = total.astype(BF16).astype(F32)
+    place = lax.broadcasted_iota(jnp.int32, (2 * VROWS, members), 0)
+    twice = jnp.concatenate([diagonal, diagonal], axis=1)
+    tail = jnp.where(place == 0, high, jnp.where(place == 1, total - high, twice))
+    send[half:, :] = tail.astype(BF16)
+
+
+def unpacked(given):
+    half = given.shape[1] // 2
+    row, col = half_masks(half)
+    shared = given[:half, :half].astype(F32)
+    side = given[:half, half:].astype(F32)
+    tail = given[half:, :].astype(F32)
+    mirrored = shared.T
+    top = jnp.where(col >= row, shared, mirrored)
+    low = jnp.where(col < row, shared, mirrored)
+    low = jnp.where(col == row, tail[2:3, :half], low)
+    gram = jnp.concatenate(
+        [jnp.concatenate([top, side], axis=1), jnp.concatenate([side.T, low], axis=1)], axis=0
+    )
+    return gram, tail[0:1, :] + tail[1:2, :]
 
 
 def inner_kernel(
@@ -277,15 +312,17 @@
     col = lax.broadcasted_iota(jnp.int32, (members, members), 1)
     diagonal = row == col
 
-    def times(a, a_s, b, b_s):
-        product = jnp.dot(a.astype(BF16), b.astype(BF16), preferred_element_type=F32)
-        return product + a_s * b + b_s * a
+    def matmul(a, b):
+        return jnp.dot(a.astype(BF16), b.astype(BF16), preferred_element_type=F32)
+
+    def times(a, b):
+        return matmul(a, b) + (a + b)
 
     totals = []
     for t, here in enumerate(grams):
         trace = jnp.sum(jnp.where(diagonal, here, 0.0)) + members * (members - 1.0)
-        scale = 1.0 / trace
-        y_dev[t] = here * scale + jnp.where(diagonal, (members - 1.0) * scale - 1.0 / members, 0.0)
+        scale = members / trace
+        y_dev[t] = here * scale + jnp.where(diagonal, (members - 1.0) * scale - 1.0, 0.0)
         totals.append(trace)
     a0, a1, a2, a3, a4 = scalar_steps()
     y_s, z_s = 1.0 / members, 1.0
@@ -295,27 +332,32 @@
         p2_s = p_s * p_s
         h_s = a2 + a3 * p_s + a4 * p2_s
         q_s = p2_s * h_s + a0 + a1 * p_s
+        h_p, h_p2 = a3 * p_s / h_s, a4 * p2_s / h_s
+        q_h, q_p = p2_s * h_s / q_s, a1 * p_s / q_s
         for t in range(patches):
-            p_dev[t] = y_dev[t] if first else times(z_dev[t], z_s, y_dev[t], y_s)
+            p_dev[t] = y_dev[t] if first else times(z_dev[t], y_dev[t])
         between()
         for t in range(patches):
-            s_dev[t] = times(p_dev[t], p_s, p_dev[t], p_s)
+            p = p_dev[t]
+            s_dev[t] = matmul(p, p) + (p + p)
         between()
         for t in range(patches):
             p, p2 = p_dev[t], s_dev[t]
-            s_dev[t] = times(p2, p2_s, a3 * p + a4 * p2, h_s) + a1 * p
+            product = matmul(p2, h_p * p + h_p2 * p2)
+            s_dev[t] = q_h * product + ((q_h * h_p + q_p) * p + (q_h + q_h * h_p2) * p2)
         for t in range(patches):
             q = s_dev[t]
             if not final:
-                y_dev[t] = times(y_dev[t], y_s, q, q_s)
-            z_dev[t] = q if first else times(z_dev[t], z_s, q, q_s)
+                y_dev[t] = times(y_dev[t], q)
+            z_dev[t] = q if first else times(z_dev[t], q)
         y_s, z_s = y_s * q_s, z_s * q_s
     for t in range(patches):
-        z = z_dev[t] + jnp.where(diagonal, z_s, 0.0)
+        z = z_dev[t] + jnp.where(diagonal, 1.0, 0.0)
         once = jnp.sum(z * vecs[t], axis=1, keepdims=True)
         twice = jnp.sum(z * once, axis=0, keepdims=True)
-        scale = lax.rsqrt(jnp.full((1, members), totals[t], F32) / (members - 1.0))
-        transform[t] = (z * scale + twice / totals[t]).astype(BF16)
+        total = jnp.full((1, members), totals[t], F32)
+        scale = z_s * lax.rsqrt(total / (members - 1.0))
+        transform[t] = (z * scale + twice * (z_s * z_s) / total).astype(BF16)
 
 
 def apply_to(transform, t, state, out, lanes):
@@ -327,18 +369,24 @@
     out[:, t, :, lanes] = result.astype(BF16).reshape(shares, local, LANES)
 
 
+def columns_of(state):
+    return [slice(first, first + LANES) for first in range(0, state.shape[3], LANES)]
+
+
 def outer_kernel(
-    inner, gram, gram_v, from_before, from_after, state, out, transform, y_dev, z_dev, p_dev, s_dev
+    inner, gram, gram_v, near, far, state, out, transform, y_dev, z_dev, p_dev, s_dev
 ):
     members = gram.shape[1]
-    patches, width = state.shape[1], state.shape[3]
+    patches = state.shape[1]
+    odd = lax.rem(lax.axis_index(RING[1]), 2)
+    sides = (1 - odd, odd)
     grams, vecs = [], []
-    for t, side in enumerate((from_before, from_after)):
-        tail = side[members:, :].astype(F32)
-        grams.append(gram[t] + side[:members, :].astype(F32))
-        vecs.append(gram_v[t, 0:1, :] + gram_v[t, 1:2, :] + tail[0:1, :] + tail[1:2, :])
-    columns = [slice(first, first + LANES) for first in range(0, width, LANES)]
-    fill = [(t, lanes) for t in range(1, patches - 1) for lanes in columns]
+    for side, given in zip(sides, (near, far)):
+        other, other_v = unpacked(given)
+        grams.append(gram[side] + other)
+        own = gram_v[side]
+        vecs.append(own[0:1, :] + own[1:2, :] + other_v)
+    fill = [(t, lanes) for t in range(1, patches - 1) for lanes in columns_of(state)]
 
     def between():
         if fill:
@@ -348,26 +396,64 @@
     root_into(transform, grams, vecs, y_dev, z_dev, p_dev, s_dev, between)
     while fill:
         between()
-    for lanes in columns:
-        for side, t in enumerate((0, patches - 1)):
-            apply_to(transform[side], t, state, out, lanes)
-
-
-def outer_call(inner, gram, gram_v, from_before, from_after, state):
+    for lanes in columns_of(state):
+        for number, side in enumerate(sides):
+            apply_to(transform[number], side * (patches - 1), state, out, lanes)
+
+
+def outer_call(inner, gram, gram_v, near, far, state):
     patches, members, _ = gram.shape
     dev = pltpu.VMEM((patches, members, members), F32)
     return pl.pallas_call(
         outer_kernel,
         name="outer",
-        out_shape=jax.ShapeDtypeStruct(state.shape, BF16),
+        out_shape=pltpu.VMEM(state.shape, BF16),
         scratch_shapes=[pltpu.VMEM((patches, members, members), BF16)] + [dev] * 4,
-        compiler_params=pltpu.CompilerParams(vmem_limit_bytes=40 << 20),
+        compiler_params=pltpu.CompilerParams(vmem_limit_bytes=MOST_VMEM),
         cost_estimate=pl.CostEstimate(
-            flops=17 * patches * 2 * members**3 + 2 * members * state.size,
-            bytes_accessed=4 * state.size,
+            flops=17 * patches * 2 * members**3 + members * state.size,
+            bytes_accessed=2 * state.size,
             transcendentals=0,
         ),
-    )(inner, gram, gram_v, from_before, from_after, state)
+    )(inner, gram, gram_v, near, far, state)
+
+
+def by_member_kernel(given, out, rows_out, sems):
+    pieces, _, step, width = rows_out.shape
+
+    def put(piece):
+        return pltpu.make_async_copy(
+            rows_out.at[piece], out.at[:, pl.ds(piece * step, step)], sems.at[piece]
+        )
+
+    for piece in range(pieces):
+        for first in range(0, width, LANES):
+            lanes = slice(first, first + LANES)
+            for row in range(0, step, 8):
+                place = piece * step + row
+                block = given[place : place + 8, :, lanes]
+                rows_out[piece, :, row : row + 8, lanes] = jnp.swapaxes(block, 0, 1)
+        put(piece).start()
+    for piece in range(pieces):
+        put(piece).wait()
+
+
+def by_member_call(given):
+    group_patches, local, width = given.shape
+    pieces, step = 8, group_patches // 8
+    return pl.pallas_call(
+        by_member_kernel,
+        name="by_member",
+        out_shape=jax.ShapeDtypeStruct((local, group_patches, width), BF16),
+        in_specs=[pl.BlockSpec(memory_space=pltpu.VMEM)],
+        out_specs=pl.BlockSpec(memory_space=pltpu.HBM),
+        scratch_shapes=[
+            pltpu.VMEM((pieces, local, step, width), BF16),
+            pltpu.SemaphoreType.DMA((pieces,)),
+        ],
+        compiler_params=pltpu.CompilerParams(vmem_limit_bytes=MOST_VMEM),
+        cost_estimate=pl.CostEstimate(flops=0, bytes_accessed=4 * given.size, transcendentals=0),
+    )(given)
 
 
 def on_device(background, obs_pert, obs_innov, obs_rinv, obs_pos, obs_count):
@@ -380,10 +466,10 @@
     given = (obs_count, obs_pert, fields)
     state = lax.all_to_all(by_patch, "mem", split_axis=0, concat_axis=0, tiled=True)
     state = state.reshape(shares, patches, local, width)
-    to_before, to_after = gram_call(
+    to_near, to_far = gram_call(
         edge_kernel,
         "edge",
-        [pltpu.VMEM((members + 2 * VROWS, members), BF16)] * 2,
+        [pltpu.VMEM((members // 2 + 2 * VROWS, members), BF16)] * 2,
         1,
         2,
         2 * pieces,
@@ -392,10 +478,10 @@
         *given,
     )
     size = lax.axis_size(RING)
-    up = [(i, (i + 1) % size) for i in range(size)]
-    down = [(j, i) for i, j in up]
-    from_after = lax.ppermute(to_before, RING, down)
-    from_before = lax.ppermute(to_after, RING, up)
+    from_near = lax.ppermute(to_near, RING, [(i, i ^ 1) for i in range(size)])
+    from_far = lax.ppermute(
+        to_far, RING, [(i, (i + 1 if i % 2 else i - 1) % size) for i in range(size)]
+    )
     inner, gram, gram_v = gram_call(
         inner_kernel,
         "inner",
@@ -411,10 +497,10 @@
         10 * matmul,
         *given,
     )
-    result = outer_call(inner, gram, gram_v, from_before, from_after, state)
+    result = outer_call(inner, gram, gram_v, from_near, from_far, state)
     result = result.reshape(group_patches, local, width)
     result = lax.all_to_all(result, "mem", split_axis=0, concat_axis=0, tiled=True)
-    return jnp.swapaxes(result, 0, 1)
+    return by_member_call(result)
 
 
 def solution(mesh):

time: 55.6 us -> 53.8 us (0.968)
  starting transfers between devices: 13.1 us -> 11.4 us
  local copies, waits for them, and re-layouts: 1.55 us -> 0 us
  waiting for transfers between devices: 3.5 us -> 4.78 us
  Pallas kernels: 15 us -> 16.1 us
  blocking collectives: 22.1 us -> 21.2 us
    ppermute x2, starting transfers between devices: 6.05 us -> 4.33 us  [the longest x1 2.33 us: on_device(): lax.ppermute(to_far, RING, [(i, (i + 1 if i % 2 else i - 1) % size) for i...]
    transpose x1 -> x0, local copies, waits for them, and re-layouts: 1.55 us -> none  [on_device(): return jnp.swapaxes(result, 0, 1)]
    pallas_call x1 -> x2, Pallas kernels: 3.96 us -> 5.06 us  [the longest x1 3.99 us: outer_call(): pl.pallas_call(outer_kernel, name='outer', out_shape=pltpu.VMEM(state.sha...]
    all_to_all x1, blocking collectives: 22.1 us -> 21.2 us  [on_device(): lax.all_to_all(result, 'mem', split_axis=0, concat_axis=0, tiled=True)]
    all_to_all x1, waiting for transfers between devices: 2 us -> 2.92 us  [on_device(): lax.all_to_all(by_patch, 'mem', split_axis=0, concat_axis=0, tiled=True)]
  transfers between devices with their start and end apart: 3 -> 3, of which waited for: 2 -> 2; matrix products, arithmetic and copies ran while one was open for 0% -> 0% of each run, Pallas kernels for 16% -> 17%
where the time goes in v2:
time: 53.8 us; the launch traced here: 53.5 us
  blocking collectives  21.2 us (39%)
  Pallas kernels  16.1 us (30%)
  starting transfers between devices  11.4 us (21%)
  waiting for transfers between devices  4.78 us (9%)
    all_to_all x1, blocking collectives, on_device(): lax.all_to_all(result, 'mem', split_axis=0, concat_axis=0, tiled=True)  21.2 us
    pallas_call x2, Pallas kernels, gram_call(): pl.pallas_call(kernel, name=name, out_shape=outs, in_specs=[hbm, hbm, vme...  8.91 us
    all_to_all x1, starting transfers between devices, on_device(): lax.all_to_all(by_patch, 'mem', split_axis=0, concat_axis=0, tiled=True)  7.05 us
    pallas_call x1, Pallas kernels, outer_call(): pl.pallas_call(outer_kernel, name='outer', out_shape=pltpu.VMEM(state.sha...  3.99 us
    all_to_all x1, waiting for transfers between devices, on_device(): lax.all_to_all(by_patch, 'mem', split_axis=0, concat_axis=0, tiled=True)  2.92 us
    ppermute x1, starting transfers between devices, on_device(): lax.ppermute(to_far, RING, [(i, (i + 1 if i % 2 else i - 1) % size) for i...  2.33 us
    pallas_call x1, Pallas kernels, by_patch_call(): pl.pallas_call(by_patch_kernel, name='by_patch', out_shape=[jax.ShapeDtyp...  2.17 us
    ppermute x1, starting transfers between devices, on_device(): from_near = lax.ppermute(to_near, RING, [(i, i ^ 1) for i in range(size)])  2 us
  transfers between devices with their start and end apart: 3, of which 2 were waited for; matrix products, arithmetic and copies ran while one was open for 0% of the time, Pallas kernels for 17%

profile of v2, /device:TPU:96, one launch (start us, length us, event | category | flops | bytes accessed | tf_op | source)
XLA Modules:
  0.0 53.5 jit_solution(9029979202232978855)
XLA Ops:
  0.0 2.2 %by_patch.1 = (bf16[64,16,512]{2,1,0:T(8,128)(2,1)}, f32[3,4,2048]{2,1,0:T(4,128)S(1)}) custom-call(bf16[16,64,512]{2,1,0:T(8,128)(2,1)} %back.1, bf16[4,2048]{1,0:T(4,128)(2,1)} %innov.1, bf16[4,2048]{1,0:T(4,128)(2,1)} %rinv.1, bf16[4,2048]{1,0:T(4,128)(2,1)} %pos.1), custom_call_target="tpu_custom_call" | custom-call | bytes 2097152 | tf_op jit(solution)/shard_map/by_patch/pallas_call | solution.py:159
  2.2 7.0 %all-to-all-start = ((bf16[64,16,512]{2,1,0:T(8,128)(2,1)}), bf16[64,16,512]{2,1,0:T(8,128)(2,1)S(1)}, u32[]{:S(2)}, u32[]{:S(2)}) async-start(bf16[64,16,512]{2,1,0:T(8,128)(2,1)} %get-tuple-element.18), calls=%async_computation | async-start | bytes 2097152 | tf_op jit(solution)/shard_map/all_to_all | solution.py:467
  9.2 1.9 %edge.1 = (bf16[144,256]{1,0:T(8,128)(2,1)S(1)}, bf16[144,256]{1,0:T(8,128)(2,1)S(1)}) custom-call(s32[4]{0:T(128)} %given_counts.3, bf16[4,2048,256]{2,1,0:T(8,128)(2,1)} %obs.3, f32[3,4,2048]{2,1,0:T(4,128)S(1)} %get-tuple-element.12.fields), custom_call_target="tpu_custom_call" | custom-call | flops 536870912 | bytes 2097152 | tf_op jit(solution)/shard_map/edge/pallas_call | solution.py:281
  11.2 2.0 %collective-permute-start = (bf16[144,256]{1,0:T(8,128)(2,1)S(1)}, bf16[144,256]{1,0:T(8,128)(2,1)S(1)}, u32[]{:S(2)}, u32[]{:S(2)}) collective-permute-start(bf16[144,256]{1,0:T(8,128)(2,1)S(1)} %get-tuple-element.16), channel_id=1, source_target_pairs={{0,1},{1,0},{2,3},{3,2},{4,5},{5,4},{6,7},{7,6},{8,9},{9,8},{10,11... | collective-permute-start | bytes 221192 | tf_op jit(solution)/shard_map/ppermute | solution.py:481
  13.2 2.3 %collective-permute-start.1 = (bf16[144,256]{1,0:T(8,128)(2,1)S(1)}, bf16[144,256]{1,0:T(8,128)(2,1)S(1)}, u32[]{:S(2)}, u32[]{:S(2)}) collective-permute-start(bf16[144,256]{1,0:T(8,128)(2,1)S(1)} %get-tuple-element.17), channel_id=1, source_target_pairs={{0,255},{1,2},{2,1},{3,4},{4,3},{5,6},{6,5},{7,8},{8,7},{9,10},{10... | collective-permute-start | bytes 221192 | tf_op jit(solution)/shard_map/ppermute | solution.py:482
  15.5 7.0 %inner.1 = (bf16[2,256,256]{2,1,0:T(8,128)(2,1)S(1)}, f32[2,256,256]{2,1,0:T(8,128)S(1)}, f32[2,8,256]{2,1,0:T(8,128)S(1)}) custom-call(s32[4]{0:T(128)} %given_counts.3, bf16[4,2048,256]{2,1,0:T(8,128)(2,1)} %obs.3, f32[3,4,2048]{2,1,0:T(4,128)S(1)} %get-tuple-element.12.fields), custom_call_target="tpu_custom_call" | custom-call | flops 2684354560 | bytes 2097152 | tf_op jit(solution)/shard_map/inner/pallas_call | solution.py:281
  22.5 1.9 %collective-permute-done.near = bf16[144,256]{1,0:T(8,128)(2,1)S(1)} collective-permute-done((bf16[144,256]{1,0:T(8,128)(2,1)S(1)}, bf16[144,256]{1,0:T(8,128)(2,1)S(1)}, u32[]{:S(2)}, u32[]{:S(2)}) %collective-permute-start) | collective-permute-done | bytes 73760 | tf_op jit(solution)/shard_map/ppermute | solution.py:481
  24.3 0.0 collective-permute-done.1.far
  24.4 2.9 %all-to-all-done = bf16[64,16,512]{2,1,0:T(8,128)(2,1)S(1)} async-done(((bf16[64,16,512]{2,1,0:T(8,128)(2,1)}), bf16[64,16,512]{2,1,0:T(8,128)(2,1)S(1)}, u32[]{:S(2)}, u32[]{:S(2)}) %all-to-all-start) | async-done | bytes 1048608 | tf_op jit(solution)/shard_map/all_to_all | solution.py:467
  27.3 4.0 %outer.1 = bf16[16,4,16,512]{3,2,1,0:T(8,128)(2,1)S(1)} custom-call(bf16[2,256,256]{2,1,0:T(8,128)(2,1)S(1)} %get-tuple-element.13.inner, f32[2,256,256]{2,1,0:T(8,128)S(1)} %get-tuple-element.14.gram, f32[2,8,256]{2,1,0:T(8,128)S(1)} %get-tuple-element.15.gram_v, bf16[144,256]{1,0:T(8,128)(2,1)S(1)} %collective-permute-done.near, ...), custom_call_target="tpu_custom_call" | custom-call | flops 1275068416 | bytes 1048576 | tf_op jit(solution)/shard_map/outer/pallas_call | solution.py:407
  31.3 21.2 %all_to_all.10.given = bf16[64,16,512]{2,1,0:T(8,128)(2,1)S(1)} all-to-all(bf16[64,16,512]{2,1,0:T(8,128)(2,1)S(1)} %bitcast.3), channel_id=1, replica_groups=mesh['grp'=16,'mem'=16] {'mem'}, dimensions={0} | all-to-all | bytes 2097152 | tf_op jit(solution)/shard_map/all_to_all | solution.py:502
  52.5 1.1 %by_member.1 = bf16[16,64,512]{2,1,0:T(8,128)(2,1)} custom-call(bf16[64,16,512]{2,1,0:T(8,128)(2,1)S(1)} %all_to_all.10.given), custom_call_target="tpu_custom_call" | custom-call | bytes 2097152 | tf_op jit(solution)/shard_map/by_member/pallas_call | solution.py:444
Async XLA Ops:
  2.2 25.1 %all-to-all-start = ((bf16[64,16,512]{2,1,0:T(8,128)(2,1)}), bf16[64,16,512]{2,1,0:T(8,128)(2,1)S(1)}, u32[]{:S(2)}, u32[]{:S(2)}) async-start(bf16[64,16,512]{2,1,0:T(8,128)(2,1)} %get-tuple-element.18), calls=%async_computation | async-start | bytes 2097152 | tf_op jit(solution)/shard_map/all_to_all | solution.py:467
  11.2 13.2 %collective-permute-start = (bf16[144,256]{1,0:T(8,128)(2,1)S(1)}, bf16[144,256]{1,0:T(8,128)(2,1)S(1)}, u32[]{:S(2)}, u32[]{:S(2)}) collective-permute-start(bf16[144,256]{1,0:T(8,128)(2,1)S(1)} %get-tuple-element.16), channel_id=1, source_target_pairs={{0,1},{1,0},{2,3},{3,2},{4,5},{5,4},{6,7},{7,6},{8,9},{9,8},{10,11... | collective-permute-start | bytes 221192 | tf_op jit(solution)/shard_map/ppermute | solution.py:481
  13.2 11.2 %collective-permute-start.1 = (bf16[144,256]{1,0:T(8,128)(2,1)S(1)}, bf16[144,256]{1,0:T(8,128)(2,1)S(1)}, u32[]{:S(2)}, u32[]{:S(2)}) collective-permute-start(bf16[144,256]{1,0:T(8,128)(2,1)S(1)} %get-tuple-element.17), channel_id=1, source_target_pairs={{0,255},{1,2},{2,1},{3,4},{4,3},{5,6},{6,5},{7,8},{8,7},{9,10},{10... | collective-permute-start | bytes 221192 | tf_op jit(solution)/shard_map/ppermute | solution.py:482

commit v3 on v2

--- a/solution.py
+++ b/solution.py
@@ -1,3 +1,4 @@
+import functools
 import jax
 import jax.numpy as jnp
 from jax import lax
@@ -12,6 +13,7 @@
 RING = ("grp", "mem")
 VROWS = 8
 LANES = 128
+WIDE = 256
 MOST_VMEM = 40 << 20
 F32 = jnp.float32
 BF16 = jnp.bfloat16
@@ -113,21 +115,37 @@
     lax.fori_loop(0, 2 * per_patch, body, 0)
 
 
+def share_place(share, shares):
+    flip = lax.rem(lax.axis_index(RING[0]), 2)
+    return share + flip * (shares - 1 - 2 * share)
+
+
 def by_patch_kernel(
     back, innov, rinv, pos, turned, fields, rows_in, rows_out, narrow, in_sems, out_sems, sems
 ):
     step = rows_in.shape[2]
     pieces = rows_in.shape[0]
+    group_patches, patches = back.shape[1], innov.shape[0]
 
     def fetch(piece):
         return pltpu.make_async_copy(
             back.at[:, pl.ds(piece * step, step)], rows_in.at[piece], in_sems.at[piece]
         )
 
+    shares, share = group_patches // patches, patches
+
     def put(piece):
-        return pltpu.make_async_copy(
-            rows_out.at[piece], turned.at[pl.ds(piece * step, step)], out_sems.at[piece]
-        )
+        copies = []
+        for part in range(step // share):
+            place = share_place(piece * (step // share) + part, shares)
+            copies.append(
+                pltpu.make_async_copy(
+                    rows_out.at[piece, pl.ds(part * share, share)],
+                    turned.at[pl.ds(place * share, share)],
+                    out_sems.at[piece * (step // share) + part],
+                )
+            )
+        return copies
 
     for piece in range(pieces):
         fetch(piece).start()
@@ -144,12 +162,14 @@
             for row in range(0, step, 8):
                 block = rows_in[piece, :, row : row + 8, lanes]
                 rows_out[piece, row : row + 8, :, lanes] = jnp.swapaxes(block, 0, 1)
-        put(piece).start()
+        for copy in put(piece):
+            copy.start()
     for number, load in enumerate(loads):
         load.wait()
         fields[number] = narrow[number].astype(F32)
     for piece in range(pieces):
-        put(piece).wait()
+        for copy in put(piece):
+            copy.wait()
 
 
 def by_patch_call(background, innov, rinv, pos):
@@ -170,7 +190,7 @@
             pltpu.VMEM((pieces, step, local, width), BF16),
             pltpu.VMEM((3,) + innov.shape, BF16),
             pltpu.SemaphoreType.DMA((pieces,)),
-            pltpu.SemaphoreType.DMA((pieces,)),
+            pltpu.SemaphoreType.DMA((group_patches // innov.shape[0],)),
             pltpu.SemaphoreType.DMA((3,)),
         ],
         compiler_params=pltpu.CompilerParams(vmem_limit_bytes=MOST_VMEM),
@@ -347,9 +367,14 @@
             s_dev[t] = q_h * product + ((q_h * h_p + q_p) * p + (q_h + q_h * h_p2) * p2)
         for t in range(patches):
             q = s_dev[t]
-            if not final:
-                y_dev[t] = times(y_dev[t], q)
-            z_dev[t] = q if first else times(z_dev[t], q)
+            if first or final:
+                if not final:
+                    y_dev[t] = times(y_dev[t], q)
+                z_dev[t] = q if first else times(z_dev[t], q)
+            else:
+                both = matmul(jnp.concatenate([y_dev[t], z_dev[t]], axis=0), q)
+                y_dev[t] = both[:members] + (y_dev[t] + q)
+                z_dev[t] = both[members:] + (z_dev[t] + q)
         y_s, z_s = y_s * q_s, z_s * q_s
     for t in range(patches):
         z = z_dev[t] + jnp.where(diagonal, 1.0, 0.0)
@@ -362,15 +387,18 @@
 
 def apply_to(transform, t, state, out, lanes):
     shares, _, local, _ = state.shape
-    wide = state[:, t, :, lanes].astype(F32).reshape(shares * local, LANES)
+    parts = [state[share_place(share, shares), t, :, lanes] for share in range(shares)]
+    wide = jnp.concatenate(parts, axis=0).astype(F32)
     center = jnp.sum(wide, axis=0, keepdims=True) * (1.0 / (shares * local))
     spread = (wide - center).astype(BF16)
     result = jnp.dot(transform, spread, preferred_element_type=F32) + center
-    out[:, t, :, lanes] = result.astype(BF16).reshape(shares, local, LANES)
+    result = result.astype(BF16)
+    for share in range(shares):
+        out[share_place(share, shares), t, :, lanes] = result[share * local : (share + 1) * local]
 
 
 def columns_of(state):
-    return [slice(first, first + LANES) for first in range(0, state.shape[3], LANES)]
+    return [slice(first, first + WIDE) for first in range(0, state.shape[3], WIDE)]
 
 
 def outer_kernel(
@@ -418,8 +446,9 @@
     )(inner, gram, gram_v, near, far, state)
 
 
-def by_member_kernel(given, out, rows_out, sems):
+def by_member_kernel(shares, given, out, rows_out, sems):
     pieces, _, step, width = rows_out.shape
+    share = given.shape[0] // shares
 
     def put(piece):
         return pltpu.make_async_copy(
@@ -430,19 +459,27 @@
         for first in range(0, width, LANES):
             lanes = slice(first, first + LANES)
             for row in range(0, step, 8):
-                place = piece * step + row
-                block = given[place : place + 8, :, lanes]
+                first_share = (piece * step + row) // share
+                block = jnp.concatenate(
+                    [
+                        given[
+                            pl.ds(share_place(first_share + part, shares) * share, share), :, lanes
+                        ]
+                        for part in range(8 // share)
+                    ],
+                    axis=0,
+                )
                 rows_out[piece, :, row : row + 8, lanes] = jnp.swapaxes(block, 0, 1)
         put(piece).start()
     for piece in range(pieces):
         put(piece).wait()
 
 
-def by_member_call(given):
+def by_member_call(shares, given):
     group_patches, local, width = given.shape
     pieces, step = 8, group_patches // 8
     return pl.pallas_call(
-        by_member_kernel,
+        functools.partial(by_member_kernel, shares),
         name="by_member",
         out_shape=jax.ShapeDtypeStruct((local, group_patches, width), BF16),
         in_specs=[pl.BlockSpec(memory_space=pltpu.VMEM)],
@@ -464,7 +501,13 @@
     matmul = 2 * slots * members * members
     by_patch, fields = by_patch_call(background, obs_innov, obs_rinv, obs_pos)
     given = (obs_count, obs_pert, fields)
-    state = lax.all_to_all(by_patch, "mem", split_axis=0, concat_axis=0, tiled=True)
+    orders = [
+        [group * shares + (shares - 1 - place if group % 2 else place) for place in range(shares)]
+        for group in range(lax.axis_size(RING[0]))
+    ]
+    state = lax.all_to_all(
+        by_patch, RING, split_axis=0, concat_axis=0, axis_index_groups=orders, tiled=True
+    )
     state = state.reshape(shares, patches, local, width)
     to_near, to_far = gram_call(
         edge_kernel,
@@ -499,8 +542,10 @@
     )
     result = outer_call(inner, gram, gram_v, from_near, from_far, state)
     result = result.reshape(group_patches, local, width)
-    result = lax.all_to_all(result, "mem", split_axis=0, concat_axis=0, tiled=True)
-    return by_member_call(result)
+    result = lax.all_to_all(
+        result, RING, split_axis=0, concat_axis=0, axis_index_groups=orders, tiled=True
+    )
+    return by_member_call(shares, result)
 
 
 def solution(mesh):

time: 53.8 us -> 51.5 us (0.957)
  starting transfers between devices: 11.4 us -> 9.26 us
  blocking collectives: 21.2 us -> 20.2 us
  waiting for transfers between devices: 4.78 us -> 5.5 us
    ppermute x1, waiting for transfers between devices: 1.85 us -> 5.5 us  [on_device(): from_near = lax.ppermute(to_near, RING, [(i, i ^ 1) for i in range(size)])]
    all_to_all x1, waiting for transfers between devices: 2.92 us -> 0.01 us  [on_device(): lax.all_to_all(by_patch, RING, split_axis=0, concat_axis=0, axis_index_gr...]
    ppermute x1, starting transfers between devices: 2.33 us -> 0.21 us  [on_device(): lax.ppermute(to_far, RING, [(i, (i + 1 if i % 2 else i - 1) % size) for i...]
    all_to_all x1, blocking collectives: 21.2 us -> 20.2 us  [on_device(): lax.all_to_all(result, RING, split_axis=0, concat_axis=0, axis_index_grou...]
  transfers between devices with their start and end apart: 3 -> 3, of which waited for: 2 -> 1; matrix products, arithmetic and copies ran while one was open for 0% -> 0% of each run, Pallas kernels for 17% -> 17%
where the time goes in v3:
time: 51.5 us; the launch traced here: 51.2 us
  blocking collectives  20.2 us (39%)
  Pallas kernels  16.1 us (31%)
  starting transfers between devices  9.26 us (18%)
  waiting for transfers between devices  5.5 us (11%)
    all_to_all x1, blocking collectives, on_device(): lax.all_to_all(result, RING, split_axis=0, concat_axis=0, axis_index_grou...  20.2 us
    pallas_call x2, Pallas kernels, gram_call(): pl.pallas_call(kernel, name=name, out_shape=outs, in_specs=[hbm, hbm, vme...  8.92 us
    all_to_all x1, starting transfers between devices, on_device(): lax.all_to_all(by_patch, RING, split_axis=0, concat_axis=0, axis_index_gr...  7.05 us
    ppermute x1, waiting for transfers between devices, on_device(): from_near = lax.ppermute(to_near, RING, [(i, i ^ 1) for i in range(size)])  5.5 us
    pallas_call x1, Pallas kernels, outer_call(): pl.pallas_call(outer_kernel, name='outer', out_shape=pltpu.VMEM(state.sha...  3.91 us
    pallas_call x1, Pallas kernels, by_patch_call(): pl.pallas_call(by_patch_kernel, name='by_patch', out_shape=[jax.ShapeDtyp...  2.24 us
    ppermute x1, starting transfers between devices, on_device(): from_near = lax.ppermute(to_near, RING, [(i, i ^ 1) for i in range(size)])  2 us
    pallas_call x1, Pallas kernels, by_member_call(): pl.pallas_call(functools.partial(by_member_kernel, shares), name='by_memb...  1.07 us
  transfers between devices with their start and end apart: 3, of which 1 were waited for; matrix products, arithmetic and copies ran while one was open for 0% of the time, Pallas kernels for 17%

profile of v3, /device:TPU:96, one launch (start us, length us, event | category | flops | bytes accessed | tf_op | source)
XLA Modules:
  0.0 51.2 jit_solution(2821541339640166530)
XLA Ops:
  0.0 2.2 %by_patch.1 = (bf16[64,16,512]{2,1,0:T(8,128)(2,1)}, f32[3,4,2048]{2,1,0:T(4,128)S(1)}) custom-call(bf16[16,64,512]{2,1,0:T(8,128)(2,1)} %back.1, bf16[4,2048]{1,0:T(4,128)(2,1)} %innov.1, bf16[4,2048]{1,0:T(4,128)(2,1)} %rinv.1, bf16[4,2048]{1,0:T(4,128)(2,1)} %pos.1), custom_call_target="tpu_custom_call" | custom-call | bytes 2097152 | tf_op jit(solution)/shard_map/by_patch/pallas_call | solution.py:179
  2.2 7.0 %all-to-all-start = ((bf16[64,16,512]{2,1,0:T(8,128)(2,1)}), bf16[64,16,512]{2,1,0:T(8,128)(2,1)S(1)}, u32[]{:S(2)}, u32[]{:S(2)}) async-start(bf16[64,16,512]{2,1,0:T(8,128)(2,1)} %get-tuple-element.18), calls=%async_computation | async-start | bytes 2097152 | tf_op jit(solution)/shard_map/all_to_all | solution.py:508
  9.3 1.9 %edge.1 = (bf16[144,256]{1,0:T(8,128)(2,1)S(1)}, bf16[144,256]{1,0:T(8,128)(2,1)S(1)}) custom-call(s32[4]{0:T(128)} %given_counts.3, bf16[4,2048,256]{2,1,0:T(8,128)(2,1)} %obs.3, f32[3,4,2048]{2,1,0:T(4,128)S(1)} %get-tuple-element.12.fields), custom_call_target="tpu_custom_call" | custom-call | flops 536870912 | bytes 2097152 | tf_op jit(solution)/shard_map/edge/pallas_call | solution.py:301
  11.2 2.0 %collective-permute-start = (bf16[144,256]{1,0:T(8,128)(2,1)S(1)}, bf16[144,256]{1,0:T(8,128)(2,1)S(1)}, u32[]{:S(2)}, u32[]{:S(2)}) collective-permute-start(bf16[144,256]{1,0:T(8,128)(2,1)S(1)} %get-tuple-element.16), channel_id=1, source_target_pairs={{0,1},{1,0},{2,3},{3,2},{4,5},{5,4},{6,7},{7,6},{8,9},{9,8},{10,11... | collective-permute-start | bytes 221192 | tf_op jit(solution)/shard_map/ppermute | solution.py:524
  13.3 0.2 collective-permute-start.1
  13.5 7.0 %inner.1 = (bf16[2,256,256]{2,1,0:T(8,128)(2,1)S(1)}, f32[2,256,256]{2,1,0:T(8,128)S(1)}, f32[2,8,256]{2,1,0:T(8,128)S(1)}) custom-call(s32[4]{0:T(128)} %given_counts.3, bf16[4,2048,256]{2,1,0:T(8,128)(2,1)} %obs.3, f32[3,4,2048]{2,1,0:T(4,128)S(1)} %get-tuple-element.12.fields), custom_call_target="tpu_custom_call" | custom-call | flops 2684354560 | bytes 2097152 | tf_op jit(solution)/shard_map/inner/pallas_call | solution.py:301
  20.5 5.5 %collective-permute-done.near = bf16[144,256]{1,0:T(8,128)(2,1)S(1)} collective-permute-done((bf16[144,256]{1,0:T(8,128)(2,1)S(1)}, bf16[144,256]{1,0:T(8,128)(2,1)S(1)}, u32[]{:S(2)}, u32[]{:S(2)}) %collective-permute-start) | collective-permute-done | bytes 73760 | tf_op jit(solution)/shard_map/ppermute | solution.py:524
  26.0 0.0 collective-permute-done.1.far
  26.0 0.0 all-to-all-done
  26.0 3.9 %outer.1 = bf16[16,4,16,512]{3,2,1,0:T(8,128)(2,1)S(1)} custom-call(bf16[2,256,256]{2,1,0:T(8,128)(2,1)S(1)} %get-tuple-element.13.inner, f32[2,256,256]{2,1,0:T(8,128)S(1)} %get-tuple-element.14.gram, f32[2,8,256]{2,1,0:T(8,128)S(1)} %get-tuple-element.15.gram_v, bf16[144,256]{1,0:T(8,128)(2,1)S(1)} %collective-permute-done.near, ...), custom_call_target="tpu_custom_call" | custom-call | flops 1275068416 | bytes 1048576 | tf_op jit(solution)/shard_map/outer/pallas_call | solution.py:435
  29.9 20.2 %all_to_all.10.given = bf16[64,16,512]{2,1,0:T(8,128)(2,1)S(1)} all-to-all(bf16[64,16,512]{2,1,0:T(8,128)(2,1)S(1)} %bitcast.3), channel_id=1, replica_groups={{0,1,2,3,4,5,6,7,8,9,10,11,12,13,14,15},{31,30,29,28,27,26,25,24,23,22,..., dimensions={0} | all-to-all | bytes 2097152 | tf_op jit(solution)/shard_map/all_to_all | solution.py:545
  50.1 1.1 %by_member.1 = bf16[16,64,512]{2,1,0:T(8,128)(2,1)} custom-call(bf16[64,16,512]{2,1,0:T(8,128)(2,1)S(1)} %all_to_all.10.given), custom_call_target="tpu_custom_call" | custom-call | bytes 2097152 | tf_op jit(solution)/shard_map/by_member/pallas_call | solution.py:481
Async XLA Ops:
  2.2 23.7 %all-to-all-start = ((bf16[64,16,512]{2,1,0:T(8,128)(2,1)}), bf16[64,16,512]{2,1,0:T(8,128)(2,1)S(1)}, u32[]{:S(2)}, u32[]{:S(2)}) async-start(bf16[64,16,512]{2,1,0:T(8,128)(2,1)} %get-tuple-element.18), calls=%async_computation | async-start | bytes 2097152 | tf_op jit(solution)/shard_map/all_to_all | solution.py:508
  11.2 14.7 %collective-permute-start = (bf16[144,256]{1,0:T(8,128)(2,1)S(1)}, bf16[144,256]{1,0:T(8,128)(2,1)S(1)}, u32[]{:S(2)}, u32[]{:S(2)}) collective-permute-start(bf16[144,256]{1,0:T(8,128)(2,1)S(1)} %get-tuple-element.16), channel_id=1, source_target_pairs={{0,1},{1,0},{2,3},{3,2},{4,5},{5,4},{6,7},{7,6},{8,9},{9,8},{10,11... | collective-permute-start | bytes 221192 | tf_op jit(solution)/shard_map/ppermute | solution.py:524
  13.3 12.7 %collective-permute-start.1 = (bf16[144,256]{1,0:T(8,128)(2,1)S(1)}, bf16[144,256]{1,0:T(8,128)(2,1)S(1)}, u32[]{:S(2)}, u32[]{:S(2)}) collective-permute-start(bf16[144,256]{1,0:T(8,128)(2,1)S(1)} %get-tuple-element.17), channel_id=1, source_target_pairs={{0,255},{1,2},{2,1},{3,4},{4,3},{5,6},{6,5},{7,8},{8,7},{9,10},{10... | collective-permute-start | bytes 221192 | tf_op jit(solution)/shard_map/ppermute | solution.py:525

commit v4 on v3

--- a/solution.py
+++ b/solution.py
@@ -1,4 +1,5 @@
 import functools
+import math
 import jax
 import jax.numpy as jnp
 from jax import lax
@@ -115,9 +116,15 @@
     lax.fori_loop(0, 2 * per_patch, body, 0)
 
 
+def exchange_orders(shares):
+    side = math.isqrt(shares)
+    spread = [x + side * ((x + y) % side) for y in range(side) for x in range(side)]
+    return spread, spread[::-1]
+
+
 def share_place(share, shares):
-    flip = lax.rem(lax.axis_index(RING[0]), 2)
-    return share + flip * (shares - 1 - 2 * share)
+    first, second = (order.index(share) for order in exchange_orders(shares))
+    return first + lax.rem(lax.axis_index(RING[0]), 2) * (second - first)
 
 
 def by_patch_kernel(
@@ -501,8 +508,9 @@
     matmul = 2 * slots * members * members
     by_patch, fields = by_patch_call(background, obs_innov, obs_rinv, obs_pos)
     given = (obs_count, obs_pert, fields)
+    by_core = exchange_orders(shares)
     orders = [
-        [group * shares + (shares - 1 - place if group % 2 else place) for place in range(shares)]
+        [group * shares + device for device in by_core[group % 2]]
         for group in range(lax.axis_size(RING[0]))
     ]
     state = lax.all_to_all(

time: 51.5 us -> 51.9 us (level)
  the two profiles are of different devices: /device:TPU:96 before, /device:TPU:248 now
where the time goes in v4:
time: 51.9 us; the launch traced here: 52.4 us
  blocking collectives  21.2 us (41%)
  Pallas kernels  16.1 us (31%)
  starting transfers between devices  11.5 us (22%)
  waiting for transfers between devices  3.55 us (7%)
    all_to_all x1, blocking collectives, on_device(): lax.all_to_all(result, RING, split_axis=0, concat_axis=0, axis_index_grou...  21.2 us
    pallas_call x2, Pallas kernels, gram_call(): pl.pallas_call(kernel, name=name, out_shape=outs, in_specs=[hbm, hbm, vme...  8.91 us
    all_to_all x1, starting transfers between devices, on_device(): lax.all_to_all(by_patch, RING, split_axis=0, concat_axis=0, axis_index_gr...  7.18 us
    pallas_call x1, Pallas kernels, outer_call(): pl.pallas_call(outer_kernel, name='outer', out_shape=pltpu.VMEM(state.sha...  3.9 us
    all_to_all x1, waiting for transfers between devices, on_device(): lax.all_to_all(by_patch, RING, split_axis=0, concat_axis=0, axis_index_gr...  3.26 us
    ppermute x1, starting transfers between devices, on_device(): lax.ppermute(to_far, RING, [(i, (i + 1 if i % 2 else i - 1) % size) for i...  2.81 us
    pallas_call x1, Pallas kernels, by_patch_call(): pl.pallas_call(by_patch_kernel, name='by_patch', out_shape=[jax.ShapeDtyp...  2.24 us
    ppermute x1, starting transfers between devices, on_device(): from_near = lax.ppermute(to_near, RING, [(i, i ^ 1) for i in range(size)])  1.55 us
  transfers between devices with their start and end apart: 3, of which 2 were waited for; matrix products, arithmetic and copies ran while one was open for 0% of the time, Pallas kernels for 17%

profile of v4, /device:TPU:248, one launch (start us, length us, event | category | flops | bytes accessed | tf_op | source)
XLA Modules:
  0.0 52.4 jit_solution(14910660628516307963)
XLA Ops:
  0.0 2.2 %by_patch.1 = (bf16[64,16,512]{2,1,0:T(8,128)(2,1)}, f32[3,4,2048]{2,1,0:T(4,128)S(1)}) custom-call(bf16[16,64,512]{2,1,0:T(8,128)(2,1)} %back.1, bf16[4,2048]{1,0:T(4,128)(2,1)} %innov.1, bf16[4,2048]{1,0:T(4,128)(2,1)} %rinv.1, bf16[4,2048]{1,0:T(4,128)(2,1)} %pos.1), custom_call_target="tpu_custom_call" | custom-call | bytes 2097152 | tf_op jit(solution)/shard_map/by_patch/pallas_call | solution.py:186
  2.2 7.2 %all-to-all-start = ((bf16[64,16,512]{2,1,0:T(8,128)(2,1)}), bf16[64,16,512]{2,1,0:T(8,128)(2,1)S(1)}, u32[]{:S(2)}, u32[]{:S(2)}) async-start(bf16[64,16,512]{2,1,0:T(8,128)(2,1)} %get-tuple-element.18), calls=%async_computation | async-start | bytes 2097152 | tf_op jit(solution)/shard_map/all_to_all | solution.py:516
  9.4 1.9 %edge.1 = (bf16[144,256]{1,0:T(8,128)(2,1)S(1)}, bf16[144,256]{1,0:T(8,128)(2,1)S(1)}) custom-call(s32[4]{0:T(128)} %given_counts.3, bf16[4,2048,256]{2,1,0:T(8,128)(2,1)} %obs.3, f32[3,4,2048]{2,1,0:T(4,128)S(1)} %get-tuple-element.12.fields), custom_call_target="tpu_custom_call" | custom-call | flops 536870912 | bytes 2097152 | tf_op jit(solution)/shard_map/edge/pallas_call | solution.py:308
  11.4 1.5 %collective-permute-start = (bf16[144,256]{1,0:T(8,128)(2,1)S(1)}, bf16[144,256]{1,0:T(8,128)(2,1)S(1)}, u32[]{:S(2)}, u32[]{:S(2)}) collective-permute-start(bf16[144,256]{1,0:T(8,128)(2,1)S(1)} %get-tuple-element.16), channel_id=1, source_target_pairs={{0,1},{1,0},{2,3},{3,2},{4,5},{5,4},{6,7},{7,6},{8,9},{9,8},{10,11... | collective-permute-start | bytes 221192 | tf_op jit(solution)/shard_map/ppermute | solution.py:532
  12.9 2.8 %collective-permute-start.1 = (bf16[144,256]{1,0:T(8,128)(2,1)S(1)}, bf16[144,256]{1,0:T(8,128)(2,1)S(1)}, u32[]{:S(2)}, u32[]{:S(2)}) collective-permute-start(bf16[144,256]{1,0:T(8,128)(2,1)S(1)} %get-tuple-element.17), channel_id=1, source_target_pairs={{0,255},{1,2},{2,1},{3,4},{4,3},{5,6},{6,5},{7,8},{8,7},{9,10},{10... | collective-permute-start | bytes 221192 | tf_op jit(solution)/shard_map/ppermute | solution.py:533
  15.7 7.0 %inner.1 = (bf16[2,256,256]{2,1,0:T(8,128)(2,1)S(1)}, f32[2,256,256]{2,1,0:T(8,128)S(1)}, f32[2,8,256]{2,1,0:T(8,128)S(1)}) custom-call(s32[4]{0:T(128)} %given_counts.3, bf16[4,2048,256]{2,1,0:T(8,128)(2,1)} %obs.3, f32[3,4,2048]{2,1,0:T(4,128)S(1)} %get-tuple-element.12.fields), custom_call_target="tpu_custom_call" | custom-call | flops 2684354560 | bytes 2097152 | tf_op jit(solution)/shard_map/inner/pallas_call | solution.py:308
  22.7 0.3 collective-permute-done.near
  23.0 0.0 collective-permute-done.1.far
  23.0 3.3 %all-to-all-done = bf16[64,16,512]{2,1,0:T(8,128)(2,1)S(1)} async-done(((bf16[64,16,512]{2,1,0:T(8,128)(2,1)}), bf16[64,16,512]{2,1,0:T(8,128)(2,1)S(1)}, u32[]{:S(2)}, u32[]{:S(2)}) %all-to-all-start) | async-done | bytes 1048608 | tf_op jit(solution)/shard_map/all_to_all | solution.py:516
  26.3 3.9 %outer.1 = bf16[16,4,16,512]{3,2,1,0:T(8,128)(2,1)S(1)} custom-call(bf16[2,256,256]{2,1,0:T(8,128)(2,1)S(1)} %get-tuple-element.13.inner, f32[2,256,256]{2,1,0:T(8,128)S(1)} %get-tuple-element.14.gram, f32[2,8,256]{2,1,0:T(8,128)S(1)} %get-tuple-element.15.gram_v, bf16[144,256]{1,0:T(8,128)(2,1)S(1)} %collective-permute-done.near, ...), custom_call_target="tpu_custom_call" | custom-call | flops 1275068416 | bytes 1048576 | tf_op jit(solution)/shard_map/outer/pallas_call | solution.py:442
  30.2 21.2 %all_to_all.10.given = bf16[64,16,512]{2,1,0:T(8,128)(2,1)S(1)} all-to-all(bf16[64,16,512]{2,1,0:T(8,128)(2,1)S(1)} %bitcast.3), channel_id=1, replica_groups={{0,5,10,15,4,9,14,3,8,13,2,7,12,1,6,11},{27,22,17,28,23,18,29,24,19,30,..., dimensions={0} | all-to-all | bytes 2097152 | tf_op jit(solution)/shard_map/all_to_all | solution.py:553
  51.3 1.1 %by_member.1 = bf16[16,64,512]{2,1,0:T(8,128)(2,1)} custom-call(bf16[64,16,512]{2,1,0:T(8,128)(2,1)S(1)} %all_to_all.10.given), custom_call_target="tpu_custom_call" | custom-call | bytes 2097152 | tf_op jit(solution)/shard_map/by_member/pallas_call | solution.py:488
Async XLA Ops:
  2.2 24.0 %all-to-all-start = ((bf16[64,16,512]{2,1,0:T(8,128)(2,1)}), bf16[64,16,512]{2,1,0:T(8,128)(2,1)S(1)}, u32[]{:S(2)}, u32[]{:S(2)}) async-start(bf16[64,16,512]{2,1,0:T(8,128)(2,1)} %get-tuple-element.18), calls=%async_computation | async-start | bytes 2097152 | tf_op jit(solution)/shard_map/all_to_all | solution.py:516
  11.4 11.6 %collective-permute-start = (bf16[144,256]{1,0:T(8,128)(2,1)S(1)}, bf16[144,256]{1,0:T(8,128)(2,1)S(1)}, u32[]{:S(2)}, u32[]{:S(2)}) collective-permute-start(bf16[144,256]{1,0:T(8,128)(2,1)S(1)} %get-tuple-element.16), channel_id=1, source_target_pairs={{0,1},{1,0},{2,3},{3,2},{4,5},{5,4},{6,7},{7,6},{8,9},{9,8},{10,11... | collective-permute-start | bytes 221192 | tf_op jit(solution)/shard_map/ppermute | solution.py:532
  12.9 10.1 %collective-permute-start.1 = (bf16[144,256]{1,0:T(8,128)(2,1)S(1)}, bf16[144,256]{1,0:T(8,128)(2,1)S(1)}, u32[]{:S(2)}, u32[]{:S(2)}) collective-permute-start(bf16[144,256]{1,0:T(8,128)(2,1)S(1)} %get-tuple-element.17), channel_id=1, source_target_pairs={{0,255},{1,2},{2,1},{3,4},{4,3},{5,6},{6,5},{7,8},{8,7},{9,10},{10... | collective-permute-start | bytes 221192 | tf_op jit(solution)/shard_map/ppermute | solution.py:533
